TPU v7x, 256 devices: a whole 4x4x8 slice. The times are simulated.
256 devices in a mesh: seq: 32 (over z, x), head: 8 (over y, core).
Axes of the slice: x: 4, y: 4, z: 8, core: 2. Of those that a mesh axis runs over, the one named last changes fastest.
Arguments:
- query: bfloat16 [131072, 1024], P('seq', 'head'), may hold values from -6 to 6
- key: bfloat16 [131072, 1024], P('seq', 'head'), may hold values from -6 to 6
- value: bfloat16 [131072, 1024], P('seq', 'head'), may hold values from -6 to 6
- grad_out: bfloat16 [131072, 1024], P('seq', 'head'), may hold values from -6 to 6
- random_blocks: int32 [1024, 2], P('seq'), may hold values from 0 to 1023, as said below
Outputs:
- attended: bfloat16 [131072, 1024], P('seq', 'head')
- grad_query: bfloat16 [131072, 1024], P('seq', 'head')
- grad_key: bfloat16 [131072, 1024], P('seq', 'head')
- grad_value: bfloat16 [131072, 1024], P('seq', 'head')
Inputs may be any that keep to these rules, and one draw needn't show every extreme that they name: `random_blocks`: entry [j, t] names the t-th random key block of query block j. Among the 64 entries of the query blocks of one seq shard, at most 3 name blocks of any one shard (blocks s * 32 to (s + 1) * 32 - 1), and in every shard's entries some shard is named exactly 3 times.
All inputs are finite; a program needn't handle non-finite values.
Results may differ from a plain program's by a relative error of at most 0.019.
Values may be sent and summed in bfloat16 or wider, within the bound.
No kernel may reach another device: no remote copies, remote signals or barrier semaphores. Data moves between devices by JAX's collectives and lax.ppermute only.
A program may use at most 192 MiB of HBM per device.

v0:
```python
import jax
import jax.numpy as jnp
from jax import lax
from jax.sharding import PartitionSpec as P

HEAD_DIM = 64
BLOCK = 128


def with_halo(block, sides, width):
    for axis, dim in sides:
        count = lax.axis_size(axis)
        forward = [(i, i + 1) for i in range(count - 1)]
        backward = [(target, source) for source, target in forward]
        low = lax.ppermute(
            lax.slice_in_dim(block, block.shape[dim] - width, None, axis=dim), axis, forward
        )
        high = lax.ppermute(lax.slice_in_dim(block, 0, width, axis=dim), axis, backward)
        block = jnp.concatenate([low, block, high], axis=dim)
    return block


def from_root(block, axis, source):
    block = jnp.where(lax.axis_index(axis) == source, block, jnp.zeros_like(block))
    return lax.psum(block, axis)


def log_totals(scores):
    peak = jnp.max(scores, axis=-1)
    summed = jnp.sum(jnp.exp(scores - peak[..., None]), axis=-1)
    return peak + jnp.log(summed)


def slot_layout(requests, blocks_dev, shards):
    owners = requests // blocks_dev
    inner_block = requests % blocks_dev
    owner_hits = (owners[..., None] == jnp.arange(shards, dtype=jnp.int32)).astype(jnp.int32)
    earlier = jnp.cumsum(owner_hits, axis=-2) - owner_hits
    slot_rank = jnp.sum(earlier * owner_hits, axis=-1)
    return (owners, slot_rank, inner_block)


def per_device(query, key, value, grad_out, random_blocks):
    score_scale = HEAD_DIM ** (-0.5)
    shards = lax.axis_size("seq")
    shard_id = lax.axis_index("seq")
    rows_dev, columns = query.shape
    blocks_dev = rows_dev // BLOCK
    heads_dev = columns // HEAD_DIM
    capacity = max(3, 3 * blocks_dev // shards)
    group_size = 4
    group_count = blocks_dev // group_size
    total_blocks = shards * blocks_dev
    keyval = jnp.concatenate([key, value], axis=1)
    kv_blocks = keyval.reshape(blocks_dev, BLOCK, 2 * columns)
    first_rows = (jnp.arange(rows_dev) < BLOCK)[:, None] & (shard_id == 0)
    grad_masked = jnp.where(first_rows, jnp.zeros_like(grad_out), grad_out)
    padded = with_halo(keyval, (("seq", 0),), BLOCK)
    padded_blocks = padded.reshape(blocks_dev + 2, BLOCK, 2 * columns)
    head_query, head_keyval, head_grad = (
        from_root(query[:BLOCK], "seq", 0),
        from_root(keyval[:BLOCK], "seq", 0),
        from_root(grad_out[:BLOCK], "seq", 0),
    )
    owners, slot_rank, inner_block = slot_layout(random_blocks.reshape(-1), blocks_dev, shards)
    slot_index = owners * capacity + slot_rank
    asked_for = jnp.zeros((shards * capacity,), jnp.int32).at[slot_index].set(inner_block)
    asked_for = asked_for.reshape(shards, capacity)
    wanted = lax.all_to_all(asked_for, "seq", split_axis=0, concat_axis=0, tiled=True)
    fetched = lax.all_to_all(kv_blocks[wanted], "seq", split_axis=0, concat_axis=0, tiled=True)
    picked = fetched.reshape(shards * capacity, BLOCK, 2 * columns)[slot_index]
    picked = picked.reshape(blocks_dev, 2, BLOCK, 2 * columns)
    column_block = jnp.arange(6 * BLOCK) // BLOCK

    def step(carry, inputs):
        pad_grad, column_acc = carry
        group_index, query_group, grad_group, random_group = inputs
        first_block = group_index * group_size
        window = lax.dynamic_slice_in_dim(padded_blocks, first_block, group_size + 2, 0)
        window_sets = jnp.stack([window[offset : offset + 3] for offset in range(group_size)])
        global_kv = jnp.broadcast_to(
            head_keyval.reshape(1, 1, BLOCK, 2 * columns), (group_size, 1, BLOCK, 2 * columns)
        )
        listed = jnp.concatenate([window_sets, random_group, global_kv], axis=1)
        key_tiles = listed[..., :columns].reshape(group_size, 6 * BLOCK, heads_dev, HEAD_DIM)
        value_tiles = listed[..., columns:].reshape(group_size, 6 * BLOCK, heads_dev, HEAD_DIM)
        query_tiles = query_group.reshape(group_size, BLOCK, heads_dev, HEAD_DIM)
        grad_tiles = grad_group.reshape(group_size, BLOCK, heads_dev, HEAD_DIM)
        block_number = shard_id * blocks_dev + first_block + jnp.arange(group_size)
        next_inside = block_number + 1 < total_blocks
        allowed = (column_block != 2)[None, :] | next_inside[:, None]
        scores = (
            jnp.einsum(
                "gqhe,gkhe->ghqk", query_tiles, key_tiles, preferred_element_type=jnp.float32
            )
            * score_scale
        )
        scores = jnp.where(allowed[:, None, None, :], scores, -jnp.inf)
        totals = log_totals(scores)
        weights = jnp.exp(scores - totals[..., None])
        weights_low = weights.astype(jnp.bfloat16)
        attended = jnp.einsum(
            "ghqk,gkhe->gqhe", weights_low, value_tiles, preferred_element_type=jnp.float32
        ).astype(jnp.bfloat16)
        row_dots = jnp.sum(
            grad_tiles.astype(jnp.float32) * lax.optimization_barrier(attended).astype(jnp.float32),
            axis=-1,
        ).transpose(0, 2, 1)
        grad_weights = jnp.einsum(
            "gqhe,gkhe->ghqk", grad_tiles, value_tiles, preferred_element_type=jnp.float32
        )
        grad_scores = (weights * (grad_weights - row_dots[..., None])).astype(jnp.bfloat16)
        grad_rows = (
            jnp.einsum(
                "ghqk,gkhe->gqhe", grad_scores, key_tiles, preferred_element_type=jnp.float32
            )
            * score_scale
        ).astype(jnp.bfloat16)
        key_count = 6
        key_terms = (
            jnp.einsum(
                "ghqk,gqhe->gkhe", grad_scores, query_tiles, preferred_element_type=jnp.float32
            )
            * score_scale
        )
        value_terms = jnp.einsum(
            "ghqk,gqhe->gkhe", weights_low, grad_tiles, preferred_element_type=jnp.float32
        )
        terms = jnp.concatenate(
            [
                key_terms.reshape(group_size, key_count, BLOCK, columns),
                value_terms.reshape(group_size, key_count, BLOCK, columns),
            ],
            axis=-1,
        )
        local_sum = jnp.zeros((group_size + 2, BLOCK, 2 * columns), jnp.float32)
        for offset in range(group_size):
            local_sum = local_sum.at[offset : offset + 3].add(terms[offset, 0:3])
        current = lax.dynamic_slice_in_dim(pad_grad, first_block, group_size + 2, 0)
        pad_grad = lax.dynamic_update_slice_in_dim(pad_grad, current + local_sum, first_block, 0)
        column_acc = column_acc + jnp.sum(terms[:, key_count - 1], axis=0)
        carried = terms[:, 3:5]
        return (
            (pad_grad, column_acc),
            (
                attended.reshape(group_size * BLOCK, columns),
                grad_rows.reshape(group_size * BLOCK, columns),
                carried,
            ),
        )

    scan_inputs = (
        jnp.arange(group_count),
        query.reshape(group_count, group_size, BLOCK, columns),
        grad_masked.reshape(group_count, group_size, BLOCK, columns),
        picked.reshape(group_count, group_size, 2, BLOCK, 2 * columns),
    )
    start_carry = (
        jnp.zeros((blocks_dev + 2, BLOCK, 2 * columns), jnp.float32),
        jnp.zeros((BLOCK, 2 * columns), jnp.float32),
    )
    (pad_grad, column_acc), (attended, grad_query, carried) = lax.scan(
        step, start_carry, scan_inputs
    )
    attended = attended.reshape(rows_dev, columns)
    grad_query = grad_query.reshape(rows_dev, columns)
    query_head = head_query.reshape(BLOCK, heads_dev, HEAD_DIM)
    grad_head = head_grad.reshape(BLOCK, heads_dev, HEAD_DIM)
    key_rows = key.reshape(rows_dev, heads_dev, HEAD_DIM)
    value_rows = value.reshape(rows_dev, heads_dev, HEAD_DIM)
    far_scores = (
        jnp.einsum("qhe,khe->hqk", query_head, key_rows, preferred_element_type=jnp.float32)
        * score_scale
    )
    local_peak = jnp.max(far_scores, axis=-1)
    peak = lax.pmax(local_peak, "seq")
    summed = lax.psum(jnp.sum(jnp.exp(far_scores - peak[..., None]), axis=-1), "seq")
    far_totals = peak + jnp.log(summed)
    far_weights = jnp.exp(far_scores - far_totals[..., None])
    far_low = far_weights.astype(jnp.bfloat16)
    partial_out = jnp.einsum(
        "hqk,khe->qhe", far_low, value_rows, preferred_element_type=jnp.float32
    ).reshape(BLOCK, columns)
    head_out = lax.psum(partial_out, "seq").astype(jnp.bfloat16)
    far_dots = jnp.sum(
        grad_head.astype(jnp.float32)
        * lax.optimization_barrier(head_out)
        .astype(jnp.float32)
        .reshape(BLOCK, heads_dev, HEAD_DIM),
        axis=-1,
    ).T
    far_grad_weights = jnp.einsum(
        "qhe,khe->hqk", grad_head, value_rows, preferred_element_type=jnp.float32
    )
    far_grad_scores = (far_weights * (far_grad_weights - far_dots[..., None])).astype(jnp.bfloat16)
    head_dq = (
        jnp.einsum(
            "hqk,khe->qhe", far_grad_scores, key_rows, preferred_element_type=jnp.float32
        ).reshape(BLOCK, columns)
        * score_scale
    )
    far_dk = (
        jnp.einsum(
            "hqk,qhe->khe", far_grad_scores, query_head, preferred_element_type=jnp.float32
        ).reshape(rows_dev, columns)
        * score_scale
    )
    far_dv = jnp.einsum(
        "hqk,qhe->khe", far_low, grad_head, preferred_element_type=jnp.float32
    ).reshape(rows_dev, columns)
    head_dq_sum, column_sum = (
        lax.psum(head_dq.astype(jnp.bfloat16), "seq").astype(jnp.float32),
        lax.psum(column_acc.astype(jnp.bfloat16), "seq").astype(jnp.float32),
    )
    edges = jnp.concatenate([pad_grad[0], pad_grad[blocks_dev + 1]], axis=0)
    returned = with_halo(edges.astype(jnp.bfloat16), (("seq", 0),), BLOCK).astype(edges.dtype)
    key_total = pad_grad[1 : blocks_dev + 1]
    key_total = key_total.at[0].add(returned[:BLOCK])
    key_total = key_total.at[blocks_dev - 1].add(returned[3 * BLOCK :])
    grad_buffer = (
        jnp.zeros((shards * capacity, BLOCK, 2 * columns), jnp.float32)
        .at[slot_index]
        .set(carried.reshape(2 * blocks_dev, BLOCK, 2 * columns))
    )
    received = lax.all_to_all(
        grad_buffer.reshape(shards, capacity, BLOCK, 2 * columns).astype(jnp.bfloat16),
        "seq",
        split_axis=0,
        concat_axis=0,
        tiled=True,
    ).astype(jnp.float32)
    key_total = key_total.at[wanted.reshape(-1)].add(
        received.reshape(shards * capacity, BLOCK, 2 * columns)
    )
    key_total = key_total + jnp.concatenate([far_dk, far_dv], axis=1).reshape(
        blocks_dev, BLOCK, 2 * columns
    )
    key_total = key_total.at[0].add(jnp.where(shard_id == 0, column_sum, 0.0))
    flat_total = key_total.reshape(rows_dev, 2 * columns)
    grad_key = flat_total[:, :columns].astype(jnp.bfloat16)
    grad_value = flat_total[:, columns:].astype(jnp.bfloat16)
    attended = attended.at[:BLOCK].set(jnp.where(shard_id == 0, head_out, attended[:BLOCK]))
    grad_query = grad_query.at[:BLOCK].set(
        jnp.where(shard_id == 0, head_dq_sum.astype(jnp.bfloat16), grad_query[:BLOCK])
    )
    return (attended, grad_query, grad_key, grad_value)


def solution(mesh):
    return jax.shard_map(
        per_device,
        mesh=mesh,
        in_specs=(
            P("seq", "head"),
            P("seq", "head"),
            P("seq", "head"),
            P("seq", "head"),
            P("seq", None),
        ),
        out_specs=(P("seq", "head"), P("seq", "head"), P("seq", "head"), P("seq", "head")),
        check_vma=False,
    )
```

profile of v0, /device:TPU:2, one launch (start us, length us, event | category | flops | bytes accessed | tf_op | source)
XLA Modules:
  0.0 1630.6 jit_solution(14152586900548348114)
XLA Ops:
  10.0 11.6 all-to-all-start
  30.4 6.0 gather_fusion
  36.4 6.1 all-to-all-start.1
  52.0 168.0 %all-reduce.6.cloned.1.call-done = bf16[128,256]{1,0:T(8,128)(2,1)} async-done(((bf16[128,256]{1,0:T(8,128)(2,1)}), bf16[128,256]{1,0:T(8,128)(2,1)}) %all-reduce.6.cloned.1.call-update) | async-done | bytes 65552 | tf_op jit(solution)/shard_map/psum | solution.py:25
  230.6 592.3 %while.31 = (s32[]{:T(128)}, f32[34,128,256]{2,1,0:T(8,128)}, f32[128,256]{0,1:T(8,128)}, bf16[8,512,128]{2,1,0:T(8,128)(2,1)}, bf16[8,512,128]{2,1,0:T(8,128)(2...) while((s32[]{:T(128)}, f32[34,128,256]{2,1,0:T(8,128)}, ...), condition=%wide.region_9.10_spmd.clone, body=%wide.region_4.9_spmd.clone.sunk | while | flops 631447296 | bytes 103416232 | solution.py:162
  269.9 5.6 scatter-add.62
  276.9 5.6 scatter-add.63
  343.0 5.6 scatter-add.62
  350.0 5.6 scatter-add.63
  357.0 5.6 scatter-add.64
  423.1 5.6 scatter-add.63
  430.1 5.6 scatter-add.64
  822.9 6.1 broadcast_in_dim.104
  829.1 16.2 scatter_fusion
  845.3 8.1 convert_element_type.103
  853.4 7.2 all-to-all-start.2
  866.8 160.7 %all-reduce.10.cloned.1.call-done = (bf16[128,2,64]{0,2,1:T(8,128)(2,1)}, bf16[128,2,64]{0,2,1:T(8,128)(2,1)}) async-done(((bf16[128,2,64]{0,2,1:T(8,128)(2,1)}, bf16[128,2,64]{0,2,1:T(8,128)(2,1)}), (bf16[128,2,64]{0,2,1:T(8,128)(2,1)}, bf16[128,2,64]{0,2,1:T(8,128)(2,1)})) %all-reduce.10.cloned.1.call-update) | async-done | bytes 65552 | tf_op jit(solution)/shard_map/psum | solution.py:25
  1031.0 70.2 %pmax.7 = f32[2,128]{1,0:T(2,128)S(1)} all-reduce(f32[2,128]{1,0:T(2,128)S(1)} %get-tuple-element.488), channel_id=1, replica_groups=mesh['seq'=32,'head'=8] {'seq'}, use_global_device_ids=true, to_apply=%region_12.13 | all-reduce | flops 256 | bytes 2048 | tf_op jit(solution)/shard_map/pmax | solution.py:176
  1104.0 73.0 %psum.51 = f32[2,128]{1,0:T(2,128)S(1)} all-reduce(f32[2,128]{1,0:T(2,128)S(1)} %exponential_reduce_fusion.1), channel_id=1, replica_groups=mesh['seq'=32,'head'=8] {'seq'}, use_global_device_ids=true, to_apply=%region_14.15 | all-reduce | flops 256 | bytes 2048 | tf_op jit(solution)/shard_map/psum | solution.py:177
  1180.2 134.4 %psum.52 = bf16[128,128]{1,0:T(8,128)(2,1)S(1)} all-reduce(f32[128,128]{1,0:T(8,128)S(1)} %copy.99), channel_id=1, replica_groups=mesh['seq'=32,'head'=8] {'seq'}, use_global_device_ids=true, to_apply=%region_15.16 | all-reduce | flops 16384 | bytes 98304 | tf_op jit(solution)/shard_map/psum | solution.py:184
  1329.8 139.7 %psum.54 = bf16[128,128]{1,0:T(8,128)(2,1)S(1)} all-reduce(bf16[128,128]{1,0:T(8,128)(2,1)S(1)} %copy.103), channel_id=1, replica_groups=mesh['seq'=32,'head'=8] {'seq'}, use_global_device_ids=true, to_apply=%region_18.19 | all-reduce | flops 16384 | bytes 65536 | tf_op jit(solution)/shard_map/psum | solution.py:212
  1489.5 9.2 bitcast_convert_fusion
  1498.7 28.2 %scatter_fusion.1 = f32[32,128,256]{2,1,0:T(8,128)} fusion(f32[32,128,256]{2,1,0:T(8,128)} %maximum_add_fusion, s32[96]{0:T(128)S(1)} %fusion.37, f32[96,128,256]{2,1,0:T(8,128)} %bitcast_convert_fusion), kind=kCustom, calls=%fused_computation.4 | custom fusion | flops 3145728 | bytes 37749120 | tf_op jit(solution)/shard_map/scatter-add | solution.py:232
  1526.9 91.5 %all-reduce.8.cloned.1.call-done = bf16[128,256]{1,0:T(8,128)(2,1)} async-done(((bf16[128,256]{1,0:T(8,128)(2,1)}), bf16[128,256]{1,0:T(8,128)(2,1)}) %all-reduce.8.cloned.1.call-update) | async-done | bytes 65552 | tf_op jit(solution)/shard_map/psum | solution.py:213
  (705 shorter events, 625.2 us)
Async XLA Ops:
  10.0 20.1 %all-to-all-start = ((s32[32,1,3]{2,1,0:T(1,128)}), s32[32,1,3]{2,1,0:T(1,128)S(1)}, u32[]{:S(2)}, u32[]{:S(2)}) async-start(s32[32,1,3]{2,1,0:T(1,128)} %bitcast.5), calls=%async_computation | async-start | bytes 32768 | tf_op jit(solution)/shard_map/all_to_all | solution.py:69
  36.4 12.7 copy-start.13
  36.4 186.1 %all-to-all-start.1 = ((bf16[32,3,128,256]{3,2,1,0:T(8,128)(2,1)}), bf16[32,3,128,256]{3,2,1,0:T(8,128)(2,1)}, u32[]{:S(2)}, u32[]{:S(2)}) async-start(bf16[32,3,128,256]{3,2,1,0:T(8,128)(2,1)} %bitcast.208), calls=%async_computation.1 | async-start | bytes 12582912 | tf_op jit(solution)/shard_map/all_to_all | solution.py:70
  42.5 177.5 %all-reduce.6.cloned.1.call-start = ((), (), s32[]{:S(2)}) async-start(), calls=%async_computation.3 | async-start | bytes 131072 | tf_op jit(solution)/shard_map/psum | solution.py:25
  43.2 177.8 %collective-permute-start.1 = (bf16[128,256]{1,0:T(8,128)(2,1)S(1)}, bf16[128,256]{1,0:T(8,128)(2,1)S(1)}, u32[]{:S(2)}, u32[]{:S(2)}) collective-permute-start(bf16[128,256]{1,0:T(8,128)(2,1)S(1)} %get-tuple-element.484), channel_id=1, source_target_pairs={{8,0},{16,8},{24,16},{32,24},{40,32},{48,40},{56,48},{64,56},{72,6... | collective-permute-start | bytes 196616 | tf_op jit(solution)/shard_map/ppermute | solution.py:18
  45.5 175.5 %collective-permute-start = (bf16[128,256]{1,0:T(8,128)(2,1)S(1)}, bf16[128,256]{1,0:T(8,128)(2,1)S(1)}, u32[]{:S(2)}, u32[]{:S(2)}) collective-permute-start(bf16[128,256]{1,0:T(8,128)(2,1)S(1)} %get-tuple-element.485), channel_id=1, source_target_pairs={{0,8},{8,16},{16,24},{24,32},{32,40},{40,48},{48,56},{56,64},{64,7... | collective-permute-start | bytes 196616 | tf_op jit(solution)/shard_map/ppermute | solution.py:15
  289.5 8.1 copy-start
  289.5 8.1 copy-start.2
  362.6 8.1 copy-start
  362.6 8.1 copy-start.2
  508.6 8.0 copy-start
  508.7 8.0 copy-start.2
  654.7 8.0 copy-start
  654.7 8.0 copy-start.2
  800.7 8.0 copy-start
  853.4 9.6 copy-start.10
  853.4 636.1 %all-to-all-start.2 = ((bf16[32,3,128,256]{3,2,1,0:T(8,128)(2,1)}), bf16[32,3,128,256]{3,2,1,0:T(8,128)(2,1)}, u32[]{:S(2)}, u32[]{:S(2)}) async-start(bf16[32,3,128,256]{3,2,1,0:T(8,128)(2,1)} %bitcast.209), calls=%async_computation.2 | async-start | bytes 12582912 | tf_op jit(solution)/shard_map/all_to_all | solution.py:225
  860.7 166.9 %all-reduce.10.cloned.1.call-start = ((), (), s32[]{:S(2)}) async-start(), calls=%async_computation.5 | async-start | bytes 131072 | tf_op jit(solution)/shard_map/psum | solution.py:25
  863.0 755.4 %all-reduce.8.cloned.1.call-start = ((), (), s32[]{:S(2)}) async-start(), calls=%async_computation.4 | async-start | bytes 131072 | tf_op jit(solution)/shard_map/psum | solution.py:213
  863.6 313.5 %copy-start.4 = (bf16[4096,128]{0,1:T(8,128)(2,1)}, bf16[4096,128]{0,1:T(8,128)(2,1)S(1)}, u32[]{:S(2)}) copy-start(bf16[4096,128]{0,1:T(8,128)(2,1)S(1)} %copy.98) | copy-start | bytes 3145732
  1104.0 210.7 %copy-start.14 = (bf16[128,2,64]{0,2,1:T(8,128)(2,1)S(1)}, bf16[128,2,64]{0,2,1:T(8,128)(2,1)}, u32[]{:S(2)}) copy-start(bf16[128,2,64]{0,2,1:T(8,128)(2,1)} %get-tuple-element.468) | copy-start | bytes 98308
  1469.5 10.0 copy-start.9
  1472.1 13.7 collective-permute-start.3
  1477.4 8.5 collective-permute-start.2
  (76 other events, 335.0 us)
Sparse Core Ops, SparseCore 0:
  49.1 170.7 all-reduce.5
  865.6 161.8 all-reduce.9
  1480.4 137.9 all-reduce.7
where the time goes:
time: 1640 us; the launch traced here: 1630 us
  local copies, waits for them, and re-layouts  471 us (29%)
  waiting for transfers between devices  426 us (26%)
  blocking collectives  417 us (25%)
  other arithmetic  169 us (10%)
  matrix products  79.2 us (5%)
  starting transfers between devices  38.2 us (2%)
    psum x2, waiting for transfers between devices, from_root(): return lax.psum(block, axis)  329 us
    psum x1, blocking collectives, per_device(): lax.psum(head_dq.astype(jnp.bfloat16), 'seq').astype(jnp.float32)  140 us
    psum x1, blocking collectives, per_device(): head_out = lax.psum(partial_out, 'seq').astype(jnp.bfloat16)  134 us
    scatter-add x32, local copies, waits for them, and re-layouts, step(): local_sum = local_sum.at[offset:offset + 3].add(terms[offset, 0:3])  134 us
    psum x1, waiting for transfers between devices, per_device(): lax.psum(column_acc.astype(jnp.bfloat16), 'seq').astype(jnp.float32)  91.5 us
    psum x1, blocking collectives, per_device(): lax.psum(jnp.sum(jnp.exp(far_scores - peak[..., None]), axis=-1), 'seq')  73 us
    pmax x1, blocking collectives, per_device(): peak = lax.pmax(local_peak, 'seq')  70.2 us
    while x200, local copies, waits for them, and re-layouts  41.9 us
  transfers between devices with their start and end apart: 10, of which 4 were waited for; matrix products, arithmetic and copies ran while one was open for 5% of the time, Pallas kernels for 0%

commit v1 on v0

v1 whole, which is shorter than its diff:
```python
import functools
import math

import jax
import jax.numpy as jnp
from jax import lax
from jax.experimental import pallas as pl
from jax.experimental.pallas import tpu as pltpu
from jax.sharding import PartitionSpec as P

HEAD_DIM = 64
BLOCK = 128
CAP = 3
LOG2E = math.log2(math.e)
SCALE = HEAD_DIM**-0.5
F32 = jnp.float32
BF16 = jnp.bfloat16
VMEM_LIMIT = 52 * 1024 * 1024

in_vmem = pl.BlockSpec(memory_space=pltpu.VMEM)
in_smem = pl.BlockSpec(memory_space=pltpu.SMEM)


def params():
    return pltpu.CompilerParams(vmem_limit_bytes=VMEM_LIMIT)


def dot(a, b, a_dim, b_dim):
    return lax.dot_general(a, b, (((a_dim,), (b_dim,)), ((), ())), preferred_element_type=F32)


def low_lanes(shape):
    return lax.broadcasted_iota(jnp.int32, shape, len(shape) - 1) < HEAD_DIM


def join(a, b):
    a, b = a.astype(F32), b.astype(F32)
    low = low_lanes(a.shape)
    axis = a.ndim - 1
    first = jnp.where(low, a, pltpu.roll(b, HEAD_DIM, axis))
    second = jnp.where(low, pltpu.roll(a, HEAD_DIM, axis), b)
    return first.astype(BF16), second.astype(BF16)


def pack_kernel(q_ref, k_ref, v_ref, g_ref, qg0_ref, qg1_ref, kv0_ref, kv1_ref):
    qg0_ref[...], qg1_ref[...] = join(q_ref[...], g_ref[...])
    kv0_ref[...], kv1_ref[...] = join(k_ref[...], v_ref[...])


def ask_kernel(asked_ref, q_ref, k_ref, v_ref, g_ref, k_end_ref, v_end_ref, out_ref, up_ref, down_ref):
    extra = 4 * BLOCK // out_ref.shape[0]
    raw = jnp.concatenate([q_ref[...], k_ref[...], v_ref[...], g_ref[...]], axis=0)
    out_ref[:, :extra] = raw.reshape(out_ref.shape[0], extra, BLOCK)
    out_ref[:, extra:] = asked_ref[...]
    up_ref[0], up_ref[1] = k_end_ref[...], v_end_ref[...]
    down_ref[0], down_ref[1] = k_ref[...], v_ref[...]


def gather0_kernel(wanted_ref, kv_ref, piece_ref, out_ref):
    def copy(d, _):
        out_ref[d, :BLOCK] = kv_ref[wanted_ref[CAP * d]]
        out_ref[d, BLOCK:] = piece_ref[...]
        return 0

    lax.fori_loop(0, out_ref.shape[0], copy, 0, unroll=2)


def gather0_rest_kernel(wanted_ref, kv_ref, out_ref):
    def copy(d, _):
        out_ref[d, :BLOCK] = kv_ref[wanted_ref[CAP * d + 1]]
        out_ref[d, BLOCK:] = kv_ref[wanted_ref[CAP * d + 2]]
        return 0

    lax.fori_loop(0, out_ref.shape[0], copy, 0, unroll=2)


def gather1_kernel(wanted_ref, kv_ref, piece_ref, out_ref):
    def copy(d, _):
        for r in range(CAP):
            out_ref[d, r * BLOCK : (r + 1) * BLOCK] = kv_ref[wanted_ref[CAP * d + r]]
        out_ref[d, CAP * BLOCK :] = piece_ref[...]
        return 0

    lax.fori_loop(0, out_ref.shape[0], copy, 0, unroll=2)


def query_pair(qg):
    low = low_lanes(qg.shape)
    return jnp.concatenate(
        [jnp.where(low, qg * SCALE, 0.0).astype(BF16), jnp.where(low, 0.0, qg).astype(BF16)], axis=0
    )


def main0_kernel(
    slot_ref, edge_ref, qg_ref, kv_ref, low_ref, high_ref, one_ref, two_ref, raw_ref,
    od_ref, back_ref, acc_ref, side_ref, col_ref, pad_ref, far_ref, ret_ref,
):
    def spread(d, _):
        far_ref[CAP * d] = one_ref[d, :BLOCK]
        far_ref[CAP * d + 1] = two_ref[d, :BLOCK]
        far_ref[CAP * d + 2] = two_ref[d, BLOCK:]
        return 0

    lax.fori_loop(0, one_ref.shape[0], spread, 0)
    attend(
        0, slot_ref, edge_ref, qg_ref, kv_ref, low_ref, high_ref, far_ref, raw_ref,
        od_ref, ret_ref, acc_ref, side_ref, col_ref, pad_ref,
    )

    def collect(d, _):
        for r in range(CAP):
            back_ref[d, r * BLOCK : (r + 1) * BLOCK] = ret_ref[CAP * d + r]
        return 0

    lax.fori_loop(0, one_ref.shape[0], collect, 0)


def main1_kernel(
    slot_ref, edge_ref, qg_ref, kv_ref, low_ref, high_ref, three_ref, raw_ref, row_ref, col0_ref,
    od_ref, two_ref, one_ref, acc_ref, side_ref, pad_ref, far_ref, ret_ref, col_ref,
):
    shards, extra = one_ref.shape[0], one_ref.shape[1] - BLOCK

    def spread(d, _):
        for r in range(CAP):
            far_ref[CAP * d + r] = three_ref[d, r * BLOCK : (r + 1) * BLOCK]
        return 0

    lax.fori_loop(0, shards, spread, 0)
    attend(
        1, slot_ref, edge_ref, qg_ref, kv_ref, low_ref, high_ref, far_ref, raw_ref,
        od_ref, ret_ref, acc_ref, side_ref, col_ref, pad_ref,
    )

    def collect(d, _):
        two_ref[d, :BLOCK] = ret_ref[CAP * d]
        two_ref[d, BLOCK : 2 * BLOCK] = ret_ref[CAP * d + 1]
        one_ref[d, :BLOCK] = ret_ref[CAP * d + 2]
        return 0

    lax.fori_loop(0, shards, collect, 0)
    parts = [row_ref[0], row_ref[1], col0_ref[...], col_ref[...]]
    parts = jnp.concatenate([x.astype(BF16) for x in parts], axis=0)
    two_ref[:, 2 * BLOCK :] = parts.reshape(shards, extra, BLOCK)
    one_ref[:, BLOCK:] = jnp.zeros((shards, extra, BLOCK), BF16)


def attend(
    head, slot_ref, edge_ref, qg_ref, kv_ref, low_ref, high_ref, far_ref, raw_ref,
    od_ref, ret_ref, acc_ref, side_ref, col_ref, pad_ref,
):
    blocks = qg_ref.shape[0]
    is_first, is_last = edge_ref[0], edge_ref[1]
    first = join(raw_ref[BLOCK : 2 * BLOCK], raw_ref[2 * BLOCK : 3 * BLOCK])[head]
    pad_ref[0] = join(low_ref[0], low_ref[1])[head]
    pad_ref[blocks + 1] = join(high_ref[0], high_ref[1])[head]
    pad_ref[1 : blocks + 1] = kv_ref[...]
    acc_ref[...] = jnp.zeros_like(acc_ref)
    ret_ref[...] = jnp.zeros_like(ret_ref)
    col_ref[...] = jnp.zeros_like(col_ref)

    def step(j, _):
        slot0, slot1 = slot_ref[2 * j], slot_ref[2 * j + 1]
        keep = 1.0 - ((j == 0) & (is_first == 1)).astype(F32)
        qg = qg_ref[j].astype(F32) * keep
        pair = query_pair(qg)
        window = pad_ref[pl.ds(j, 3)].reshape(3 * BLOCK, BLOCK)
        kv = jnp.concatenate([window, far_ref[slot0], far_ref[slot1], first], axis=0)
        both = dot(kv, pair, 1, 1)
        scores, gw = both[:, :BLOCK], both[:, BLOCK:]
        drop = (j == blocks - 1) & (is_last == 1)
        bias = jnp.where(drop, -jnp.inf, 0.0).astype(F32)
        scores = jnp.concatenate(
            [scores[: 2 * BLOCK], scores[2 * BLOCK : 3 * BLOCK] + bias, scores[3 * BLOCK :]], axis=0
        )
        peak = jnp.max(scores, axis=0, keepdims=True)
        expo = jnp.exp2((scores - peak) * LOG2E)
        weights = expo * (1.0 / jnp.sum(expo, axis=0, keepdims=True))
        wlow = weights.astype(BF16)
        kvt = kv.T
        out_t = dot(kvt, wlow, 1, 0)
        rounded = out_t.astype(BF16).astype(F32)
        row_dot = jnp.sum((rounded * qg.T)[HEAD_DIM:], axis=0, keepdims=True)
        ds = (weights * (gw - row_dot)).astype(BF16)
        dq_t = dot(kvt, ds, 1, 0)
        od_t = jnp.concatenate([dq_t[:HEAD_DIM] * SCALE, out_t[HEAD_DIM:]], axis=0)
        od_ref[j] = od_t.T.astype(BF16)
        terms = dot(jnp.concatenate([ds, wlow], axis=1), pair, 1, 0)
        acc_ref[pl.ds(j, 3)] += terms[: 3 * BLOCK].reshape(3, BLOCK, BLOCK)
        ret_ref[slot0] = terms[3 * BLOCK : 4 * BLOCK].astype(BF16)
        ret_ref[slot1] = terms[4 * BLOCK : 5 * BLOCK].astype(BF16)
        col_ref[...] += terms[5 * BLOCK :]
        return 0

    lax.fori_loop(0, blocks, step, 0)
    side_ref[0] = acc_ref[0].astype(BF16)
    side_ref[1] = acc_ref[blocks + 1].astype(BF16)


def raw_query(raw_ref):
    return join(raw_ref[:BLOCK], raw_ref[3 * BLOCK :])


def two_parts(x):
    high = x.astype(BF16)
    return high, (x - high.astype(F32)).astype(BF16)


def row_forward_kernel(raw_ref, kv0_ref, kv1_ref, stats_ref, peak_ref, out_ref, *, chunk):
    rows = []
    for h, kv_ref in enumerate((kv0_ref, kv1_ref)):
        qg = raw_query(raw_ref)[h].astype(F32)
        query = query_pair(qg)[:BLOCK]

        def step(c, carry, kv_ref=kv_ref, query=query):
            peak, total, out = carry
            kv = kv_ref[pl.ds(pl.multiple_of(c * chunk, chunk), chunk)]
            scores = dot(kv, query, 1, 1)
            new = jnp.maximum(peak, jnp.max(scores, axis=0, keepdims=True))
            shrink = jnp.exp2((peak - new) * LOG2E)
            expo = jnp.exp2((scores - new) * LOG2E)
            total = total * shrink + jnp.sum(expo, axis=0, keepdims=True)
            out = out * shrink + dot(kv, expo.astype(BF16), 0, 0)
            return new, total, out

        start = (
            jnp.full((1, BLOCK), -jnp.inf, F32),
            jnp.zeros((1, BLOCK), F32),
            jnp.zeros((BLOCK, BLOCK), F32),
        )
        peak, total, out = lax.fori_loop(0, kv_ref.shape[0] // chunk, step, start)
        point = peak.astype(BF16)
        shift = jnp.exp2((peak - point.astype(F32)) * LOG2E)
        out = out * shift
        row_dot = jnp.sum((out * qg.T)[HEAD_DIM:], axis=0, keepdims=True)
        rows += [point, *two_parts(total * shift), *two_parts(row_dot)]
        peak_ref[h : h + 1] = point.astype(F32)
        out_ref[h] = out
    rows = [r.astype(F32) for r in rows] + [jnp.zeros((6, BLOCK), F32)]
    stats_ref[...] = jnp.concatenate(rows, axis=0).astype(BF16)


def row_backward_kernel(
    raw_ref, kv0_ref, kv1_ref, all_ref, peak_ref, out_ref, far0_ref, far1_ref, row_ref, *, chunk
):
    stats = all_ref[...].astype(F32)
    for h, (kv_ref, far_ref) in enumerate(((kv0_ref, far0_ref), (kv1_ref, far1_ref))):
        qg = raw_query(raw_ref)[h].astype(F32)
        pair = query_pair(qg)
        row = [stats[:, 5 * h + i] for i in range(5)]
        peak = jnp.max(row[0], axis=0, keepdims=True)
        grow = jnp.exp2((row[0] - peak) * LOG2E)
        scale = 1.0 / jnp.sum((row[1] + row[2]) * grow, axis=0, keepdims=True)
        row_dot = jnp.sum((row[3] + row[4]) * grow, axis=0, keepdims=True) * scale

        def step(c, dq_t, kv_ref=kv_ref, far_ref=far_ref, pair=pair, peak=peak, scale=scale, row_dot=row_dot):
            rows = pl.ds(pl.multiple_of(c * chunk, chunk), chunk)
            kv = kv_ref[rows]
            both = dot(kv, pair, 1, 1)
            weights = jnp.exp2((both[:, :BLOCK] - peak) * LOG2E) * scale
            ds = (weights * (both[:, BLOCK:] - row_dot)).astype(BF16)
            far_ref[rows] = dot(jnp.concatenate([ds, weights.astype(BF16)], axis=1), pair, 1, 0)
            return dq_t + dot(kv, ds, 0, 0)

        dq_t = lax.fori_loop(0, kv_ref.shape[0] // chunk, step, jnp.zeros((BLOCK, BLOCK), F32))
        out_t = out_ref[h] * (jnp.exp2((peak_ref[h : h + 1] - peak) * LOG2E) * scale)
        row_ref[h] = jnp.concatenate([dq_t[:HEAD_DIM] * SCALE, out_t[HEAD_DIM:]], axis=0).T


def add_slots(tot_ref, wanted_ref, back_ref, ranks):
    def add(d, _):
        for at, r in enumerate(ranks):
            tot_ref[wanted_ref[CAP * d + r]] += back_ref[d, at * BLOCK : (at + 1) * BLOCK].astype(F32)
        return 0

    lax.fori_loop(0, back_ref.shape[0], add, 0)


def own_rows(h, tot_ref, acc_ref, far_ref, left_ref, right_ref):
    blocks = tot_ref.shape[0]
    tot_ref[...] = acc_ref[1 : blocks + 1] + far_ref[...].reshape(tot_ref.shape)
    tot_ref[blocks - 1] += right_ref[h].astype(F32)
    tot_ref[0] += left_ref[h].astype(F32)


def total0_kernel(
    wanted_ref, acc_ref, far_ref, left_ref, right_ref, three_ref, out_ref, block_ref, tot_ref
):
    own_rows(0, tot_ref, acc_ref, far_ref, left_ref, right_ref)
    add_slots(tot_ref, wanted_ref, three_ref, range(CAP))
    block_ref[...] = tot_ref[0]
    out_ref[...] = tot_ref[...].astype(BF16)


def total1_kernel(wanted_ref, acc_ref, far_ref, left_ref, right_ref, two_ref, tot_ref):
    own_rows(1, tot_ref, acc_ref, far_ref, left_ref, right_ref)
    add_slots(tot_ref, wanted_ref, two_ref, range(2))


def last_kernel(
    wanted_ref, edge_ref, part_ref, one_ref, head0_ref, block_ref, dk_ref, dv_ref, tot_ref
):
    tot_ref[...] = part_ref[...]
    add_slots(tot_ref, wanted_ref, one_ref, range(2, CAP))
    root = one_ref[:, BLOCK:].reshape(4 * BLOCK, BLOCK).astype(F32) * edge_ref[0].astype(F32)
    tot_ref[0] += root[3 * BLOCK :]

    def write(b, _):
        dk_ref[b], dv_ref[b] = join(head0_ref[b], tot_ref[b])
        return 0

    lax.fori_loop(0, tot_ref.shape[0], write, 0, unroll=2)
    dk_ref[0], dv_ref[0] = join(block_ref[...] + root[2 * BLOCK : 3 * BLOCK], tot_ref[0])


def unpack_kernel(od0_ref, od1_ref, att_ref, dq_ref):
    def write(b, _):
        dq_ref[b], att_ref[b] = join(od0_ref[b], od1_ref[b])
        return 0

    lax.fori_loop(0, od0_ref.shape[0], write, 0)


def root_kernel(edge_ref, root_ref, att_ref, dq_ref, att_out, dq_out):
    dq, att = join(root_ref[:BLOCK], root_ref[BLOCK : 2 * BLOCK])
    is_first = edge_ref[0] == 1
    att_out[...] = jnp.where(is_first, att.astype(F32), att_ref[...].astype(F32)).astype(BF16)
    dq_out[...] = jnp.where(is_first, dq.astype(F32), dq_ref[...].astype(F32)).astype(BF16)


def in_hbm(x):
    return pltpu.with_memory_space_constraint(x, pltpu.HBM)


def call(kernel, outs, operands, smem=0, scratch=(), us=2, loose=()):
    return pl.pallas_call(
        kernel,
        out_shape=[pltpu.HBM(s, d) for s, d in outs],
        in_specs=[in_smem] * smem + [in_vmem] * (len(operands) - smem),
        out_specs=[in_vmem] * len(outs),
        scratch_shapes=[pltpu.VMEM(s, d) for s, d in scratch],
        compiler_params=params(),
        cost_estimate=pl.CostEstimate(flops=us * 10**9, transcendentals=0, bytes_accessed=10**6),
    )(*(x if i < smem or i in loose else in_hbm(x) for i, x in enumerate(operands)))


def exchange(blocks):
    return lax.all_to_all(blocks, "seq", split_axis=0, concat_axis=0, tiled=True)


def after(x, done):
    return lax.optimization_barrier((x, done))


def per_device(query, key, value, grad_out, random_blocks):
    shards, here = lax.axis_size("seq"), lax.axis_index("seq")
    rows = query.shape[0]
    blocks = rows // BLOCK
    slots = shards * CAP
    extra = 4 * BLOCK // shards
    tile = (BLOCK, BLOCK)
    grid = (blocks, *tile)
    forward = [(i, i + 1) for i in range(shards - 1)]
    backward = [(i + 1, i) for i in range(shards - 1)]

    named = random_blocks.reshape(-1)
    owners, inner = named // blocks, named % blocks
    places = jnp.arange(named.shape[0])
    same = (owners[:, None] == owners[None, :]) & (places[None, :] < places[:, None])
    slot_of = owners * CAP + jnp.sum(same.astype(jnp.int32), axis=1)
    asked = jnp.sum(
        jnp.where(slot_of[None, :] == jnp.arange(slots)[:, None], inner[None, :], 0), axis=1
    ).reshape(shards, 1, CAP)
    asked = jnp.pad(asked.astype(BF16), ((0, 0), (0, 15), (0, BLOCK - CAP)))
    top = pl.BlockSpec(tile, lambda i: (0, 0))
    end = pl.BlockSpec(tile, lambda i: (blocks - 1, 0))
    query, key, value, grad_out = (in_hbm(x) for x in (query, key, value, grad_out))
    message, up, down = pl.pallas_call(
        ask_kernel,
        grid=(1,),
        out_shape=[
            pltpu.HBM((shards, extra + 16, BLOCK), BF16),
            pltpu.HBM((2, *tile), BF16),
            pltpu.HBM((2, *tile), BF16),
        ],
        in_specs=[pl.BlockSpec(asked.shape, lambda i: (0, 0, 0)), top, top, top, top, end, end],
        out_specs=[
            pl.BlockSpec((shards, extra + 16, BLOCK), lambda i: (0, 0, 0)),
            pl.BlockSpec((2, *tile), lambda i: (0, 0, 0)),
            pl.BlockSpec((2, *tile), lambda i: (0, 0, 0)),
        ],
        compiler_params=params(),
    )(asked, query, key, value, grad_out, key, value)
    low = lax.ppermute(up, "seq", forward)
    high = lax.ppermute(down, "seq", backward)
    got = exchange(message)
    wanted = got[:, extra, :CAP].astype(jnp.int32).reshape(-1)
    edge = jnp.stack([here == 0, here == shards - 1]).astype(jnp.int32)

    chunk = 512
    part = pl.BlockSpec((chunk, BLOCK), lambda i: (i, 0))
    qg0, qg1, kv0, kv1 = pl.pallas_call(
        pack_kernel,
        grid=(rows // chunk,),
        out_shape=[pltpu.HBM((rows, BLOCK), BF16)] * 4,
        in_specs=[part] * 4,
        out_specs=[part] * 4,
        compiler_params=params(),
    )(query, key, value, grad_out)
    (one0,) = call(
        gather0_kernel,
        [((shards, BLOCK + extra, BLOCK), BF16)],
        (wanted, kv0.reshape(grid), got[0, :extra]),
        smem=1,
        loose=(2,),
    )
    (two0,) = call(
        gather0_rest_kernel,
        [((shards, 2 * BLOCK, BLOCK), BF16)],
        (wanted, kv0.reshape(grid)),
        smem=1,
    )
    one0, low, high = lax.optimization_barrier((one0, low, high))
    one0 = exchange(one0)
    two0, one0 = after(two0, one0)
    two0 = exchange(two0)
    first = one0[:, BLOCK:].reshape(4 * BLOCK, BLOCK)
    stats, peak, partial = call(
        functools.partial(row_forward_kernel, chunk=chunk),
        [((16, BLOCK), BF16), ((2, BLOCK), F32), ((2, *tile), F32)],
        (first, kv0, kv1),
        us=8,
        loose=(0,),
    )
    (three1,) = call(
        gather1_kernel,
        [((shards, CAP * BLOCK + extra, BLOCK), BF16)],
        (wanted, kv1.reshape(grid), stats),
        smem=1,
        loose=(2,),
    )
    three1, two0 = after(three1, two0)
    three1 = exchange(three1)
    scratch = [((blocks + 2, *tile), BF16), ((slots, *tile), BF16), ((slots, *tile), BF16)]
    od0, back0, acc0, side0, col0 = call(
        main0_kernel,
        [
            (grid, BF16),
            ((shards, CAP * BLOCK, BLOCK), BF16),
            ((blocks + 2, *tile), F32),
            ((2, *tile), BF16),
            (tile, F32),
        ],
        (slot_of, edge, qg0.reshape(grid), kv0.reshape(grid), low, high, one0, two0, first),
        smem=2,
        loose=(4, 5, 6, 7, 8),
        scratch=scratch,
        us=38,
    )
    back0, three1 = after(back0, three1)
    back0 = exchange(back0)
    far0, far1, row_od = call(
        functools.partial(row_backward_kernel, chunk=chunk),
        [((rows, BLOCK), F32)] * 2 + [((2, *tile), F32)],
        (first, kv0, kv1, three1[:, CAP * BLOCK :], peak, partial),
        us=8,
        loose=(0, 3),
    )
    od1, two1, one1, acc1, side1 = call(
        main1_kernel,
        [
            (grid, BF16),
            ((shards, 2 * BLOCK + extra, BLOCK), BF16),
            ((shards, BLOCK + extra, BLOCK), BF16),
            ((blocks + 2, *tile), F32),
            ((2, *tile), BF16),
        ],
        (
            slot_of, edge, qg1.reshape(grid), kv1.reshape(grid), low, high, three1, first,
            row_od, col0,
        ),
        smem=2,
        loose=(4, 5, 6, 7),
        scratch=[*scratch, (tile, F32)],
        us=38,
    )
    left = lax.ppermute(jnp.stack([side0[1], side1[1]]), "seq", forward)
    right = lax.ppermute(jnp.stack([side0[0], side1[0]]), "seq", backward)
    two1, back0, left, right = lax.optimization_barrier((two1, back0, left, right))
    two1 = exchange(two1)
    total = jnp.sum(two1[:, 2 * BLOCK :].astype(F32), axis=0).astype(BF16)
    one1 = one1.at[:, BLOCK:].set(jnp.broadcast_to(total, (shards, extra, BLOCK)))
    one1 = exchange(one1)
    attended, grad_query = call(unpack_kernel, [(grid, BF16)] * 2, (od0, od1), us=4)
    whole = [(grid, F32)]
    head0, block0 = call(
        total0_kernel,
        [(grid, BF16), (tile, F32)],
        (wanted, acc0, far0, left, right, back0),
        smem=1,
        loose=(3, 4, 5),
        scratch=whole,
        us=6,
    )
    (part1,) = call(
        total1_kernel, whole, (wanted, acc1, far1, left, right, two1), smem=1, us=4, loose=(3, 4, 5)
    )
    grad_key, grad_value = call(
        last_kernel,
        [(grid, BF16)] * 2,
        (wanted, edge, part1, one1, head0, block0),
        smem=2,
        loose=(3,),
        scratch=whole,
        us=4,
    )
    attended, grad_query, grad_key, grad_value = (
        x.reshape(rows, BLOCK) for x in (attended, grad_query, grad_key, grad_value)
    )
    root = one1[:, BLOCK:].reshape(4 * BLOCK, BLOCK)
    attended, grad_query = pl.pallas_call(
        root_kernel,
        grid=(1,),
        out_shape=[pltpu.HBM((rows, BLOCK), BF16)] * 2,
        in_specs=[in_smem, pl.BlockSpec((4 * BLOCK, BLOCK), lambda i: (0, 0)), top, top],
        out_specs=[top, top],
        input_output_aliases={2: 0, 3: 1},
        compiler_params=params(),
    )(edge, root, in_hbm(attended), in_hbm(grad_query))
    return attended, grad_query, grad_key, grad_value


def solution(mesh):
    split = P("seq", "head")
    return jax.shard_map(
        per_device,
        mesh=mesh,
        in_specs=(split, split, split, split, P("seq", None)),
        out_specs=(split, split, split, split),
        check_vma=False,
    )
```

time: 1640 us -> 383 us (0.23)
  local copies, waits for them, and re-layouts: 471 us -> 5.65 us
  blocking collectives: 417 us -> 58 us
  waiting for transfers between devices: 426 us -> 114 us
  other arithmetic: 169 us -> 0.49 us
  Pallas kernels: 0 us -> 145 us
  matrix products: 79.2 us -> 0 us
  starting transfers between devices: 38.2 us -> 58 us
    psum x3 -> x0, waiting for transfers between devices: 420 us -> none  [the longest x2 329 us: from_root(): return lax.psum(block, axis)]
    psum x3 -> x0, blocking collectives: 347 us -> none  [the longest x1 140 us: per_device(): lax.psum(head_dq.astype(jnp.bfloat16), 'seq').astype(jnp.float32)]
    pallas_call x0 -> x14, Pallas kernels: none -> 145 us  [the longest x11 135 us: call(): pl.pallas_call(kernel, out_shape=[pltpu.HBM(s, d) for s, d in outs], in_s...]
    scatter-add x32 -> x0, local copies, waits for them, and re-layouts: 134 us -> none  [step(): local_sum = local_sum.at[offset:offset + 3].add(terms[offset, 0:3])]
    all_to_all x3 -> x6, waiting for transfers between devices: 5.57 us -> 110 us  [exchange(): lax.all_to_all(blocks, 'seq', split_axis=0, concat_axis=0, tiled=True)]
    dot_general x54 -> x0, matrix products: 79.2 us -> none  [the longest x8 16.4 us: step(): jnp.einsum('ghqk,gqhe->gkhe', weights_low, grad_tiles, preferred_element_...]
    reshape x37 -> x1, local copies, waits for them, and re-layouts: 70.7 us -> 0.1 us  [per_device(): named = random_blocks.reshape(-1)]
    pmax x1 -> x0, blocking collectives: 70.2 us -> none  [per_device(): peak = lax.pmax(local_peak, 'seq')]
  transfers between devices with their start and end apart: 10 -> 10, of which waited for: 4 -> 7; matrix products, arithmetic and copies ran while one was open for 5% -> 1% of each run, Pallas kernels for 0% -> 36%
where the time goes in v1:
time: 383 us; the launch traced here: 382 us
  Pallas kernels  145 us (38%)
  waiting for transfers between devices  114 us (30%)
  starting transfers between devices  58 us (15%)
  blocking collectives  58 us (15%)
  local copies, waits for them, and re-layouts  5.65 us (1%)
    pallas_call x11, Pallas kernels, call(): pl.pallas_call(kernel, out_shape=[pltpu.HBM(s, d) for s, d in outs], in_s...  135 us
    all_to_all x6, waiting for transfers between devices, exchange(): lax.all_to_all(blocks, 'seq', split_axis=0, concat_axis=0, tiled=True)  110 us
    all_to_all x1, blocking collectives, exchange(): lax.all_to_all(blocks, 'seq', split_axis=0, concat_axis=0, tiled=True)  58 us
    all_to_all x6, starting transfers between devices, exchange(): lax.all_to_all(blocks, 'seq', split_axis=0, concat_axis=0, tiled=True)  46.3 us
  transfers between devices with their start and end apart: 10, of which 7 were waited for; matrix products, arithmetic and copies ran while one was open for 1% of the time, Pallas kernels for 36%

profile of v1, /device:TPU:2, one launch (start us, length us, event | category | flops | bytes accessed | tf_op | source)
XLA Modules:
  0.0 381.6 jit_solution(12006821772396524225)
XLA Ops:
  3.6 11.6 %all-to-all-start = ((bf16[32,32,128]{2,1,0:T(8,128)(2,1)}), bf16[32,32,128]{2,1,0:T(8,128)(2,1)S(1)}, u32[]{:S(2)}, u32[]{:S(2)}) async-start(bf16[32,32,128]{2,1,0:T(8,128)(2,1)} %get-tuple-element.62), calls=%async_computation | async-start | bytes 524288 | tf_op jit(solution)/shard_map/all_to_all | solution.py:348
  15.3 3.4 collective-permute-start
  21.1 6.9 %shard_map.84 = (bf16[4096,128]{1,0:T(8,128)(2,1)}, bf16[4096,128]{1,0:T(8,128)(2,1)}, bf16[4096,128]{1,0:T(8,128)(2,1)}, bf16[4096,128]{1,0:T(8,128)(2,1)}) custom-call(bf16[4096,128]{1,0:T(8,128)(2,1)} %q_ref.3, bf16[4096,128]{1,0:T(8,128)(2,1)} %k_end_ref.1, bf16[4096,128]{1,0:T(8,128)(2,1)} %v_end_ref.1, bf16[4096,128]{1,0:T(8,128)(2,1)} %g_ref.3), custom_call_target="tpu_custom_call" | custom-call | tf_op jit(solution)/shard_map/pallas_call | solution.py:402
  30.7 10.7 %all-to-all-start.1 = ((bf16[32,144,128]{2,1,0:T(8,128)(2,1)}), bf16[32,144,128]{2,1,0:T(8,128)(2,1)S(1)}, u32[]{:S(2)}, u32[]{:S(2)}) async-start(bf16[32,144,128]{2,1,0:T(8,128)(2,1)} %shard_map.86), calls=%async_computation.1 | async-start | bytes 2359296 | tf_op jit(solution)/shard_map/all_to_all | solution.py:348
  44.2 26.6 %all-to-all-done.1.one_ref = bf16[32,144,128]{2,1,0:T(8,128)(2,1)S(1)} async-done(((bf16[32,144,128]{2,1,0:T(8,128)(2,1)}), bf16[32,144,128]{2,1,0:T(8,128)(2,1)S(1)}, u32[]{:S(2)}, u32[]{:S(2)}) %all-to-all-start.1) | async-done | bytes 1179680 | tf_op jit(solution)/shard_map/all_to_all | solution.py:348
  70.7 6.0 %all-to-all-start.2 = ((bf16[32,256,128]{2,1,0:T(8,128)(2,1)}), bf16[32,256,128]{2,1,0:T(8,128)(2,1)S(1)}, u32[]{:S(2)}, u32[]{:S(2)}) async-start(bf16[32,256,128]{2,1,0:T(8,128)(2,1)} %shard_map.87), calls=%async_computation.2 | async-start | bytes 4194304 | tf_op jit(solution)/shard_map/all_to_all | solution.py:348
  76.7 9.6 %shard_map.88 = (bf16[16,128]{1,0:T(8,128)(2,1)}, f32[2,128]{1,0:T(2,128)}, f32[2,128,128]{2,1,0:T(8,128)}) custom-call(bf16[512,128]{1,0:T(8,128)(2,1)S(1)} %bitcast.15, bf16[4096,128]{1,0:T(8,128)(2,1)} %get-tuple-element.63.kv0_ref, bf16[4096,128]{1,0:T(8,128)(2,1)} %get-tuple-element.61.kv1_ref), custom_call_target="tpu_custom_call" | custom-call | flops 8000000000 | bytes 1000000 | tf_op jit(solution)/shard_map/pallas_call | solution.py:336
  87.0 3.3 shard_map.89
  90.3 35.3 %all-to-all-done.2.two_ref = bf16[32,256,128]{2,1,0:T(8,128)(2,1)S(1)} async-done(((bf16[32,256,128]{2,1,0:T(8,128)(2,1)}), bf16[32,256,128]{2,1,0:T(8,128)(2,1)S(1)}, u32[]{:S(2)}, u32[]{:S(2)}) %all-to-all-start.2) | async-done | bytes 2097184 | tf_op jit(solution)/shard_map/all_to_all | solution.py:348
  127.0 5.6 %all-to-all-start.3 = ((bf16[32,400,128]{2,1,0:T(8,128)(2,1)}), bf16[32,400,128]{2,1,0:T(8,128)(2,1)}, u32[]{:S(2)}, u32[]{:S(2)}) async-start(bf16[32,400,128]{2,1,0:T(8,128)(2,1)} %shard_map.89), calls=%async_computation.3 | async-start | bytes 6553600 | tf_op jit(solution)/shard_map/all_to_all | solution.py:348
  132.7 42.0 %shard_map.90 = (bf16[32,128,128]{2,1,0:T(8,128)(2,1)}, bf16[32,384,128]{2,1,0:T(8,128)(2,1)}, f32[34,128,128]{2,1,0:T(8,128)}, bf16[2,128,128]{2,1,0:T(8,128)(2,1)}, f32[128,128]{1,0:T(8,128)}) custom-call(s32[64]{0:T(128)S(1)} %multiply_add_fusion.slot_ref, s32[2]{0:T(128)S(1)} %add_convert_fusion.edge_ref, bf16[32,128,128]{2,1,0:T(8,128)(2,1)} %bitcast.27, ...), custom_call_target="tpu_custom_call" | custom-call | flops 38000001024 | bytes 1000000 | tf_op jit(solution)/shard_map/pallas_call | solution.py:336
  174.7 30.1 %all-to-all-done.3.three_ref = bf16[32,400,128]{2,1,0:T(8,128)(2,1)} async-done(((bf16[32,400,128]{2,1,0:T(8,128)(2,1)}), bf16[32,400,128]{2,1,0:T(8,128)(2,1)}, u32[]{:S(2)}, u32[]{:S(2)}) %all-to-all-start.3) | async-done | bytes 3276832 | tf_op jit(solution)/shard_map/all_to_all | solution.py:348
  204.9 6.6 %all-to-all-start.4 = ((bf16[32,384,128]{2,1,0:T(8,128)(2,1)}), bf16[32,384,128]{2,1,0:T(8,128)(2,1)}, u32[]{:S(2)}, u32[]{:S(2)}) async-start(bf16[32,384,128]{2,1,0:T(8,128)(2,1)} %get-tuple-element.83), calls=%async_computation.4 | async-start | bytes 6291456 | tf_op jit(solution)/shard_map/all_to_all | solution.py:348
  212.4 10.5 %shard_map.91 = (f32[4096,128]{1,0:T(8,128)}, f32[4096,128]{1,0:T(8,128)}, f32[2,128,128]{2,1,0:T(8,128)}) custom-call(bf16[512,128]{1,0:T(8,128)(2,1)S(1)} %bitcast.17, bf16[4096,128]{1,0:T(8,128)(2,1)} %get-tuple-element.63.kv0_ref, bf16[4096,128]{1,0:T(8,128)(2,1)} %get-tuple-element.61.kv1_ref, bf16[32,16,128]{2,1,0:T(8,128)(2,1)S(1)} %slice.55.all_ref, ...), custom_call_target="tpu_custom_call" | custom-call | flops 8000000000 | bytes 1000000 | tf_op jit(solution)/shard_map/pallas_call | solution.py:336
  222.9 42.6 %shard_map.92 = (bf16[32,128,128]{2,1,0:T(8,128)(2,1)}, bf16[32,272,128]{2,1,0:T(8,128)(2,1)}, bf16[32,144,128]{2,1,0:T(8,128)(2,1)}, f32[34,128,128]{2,1,0:T(8,128)}, bf16[2,128,128]{2,1,0:T(8,128)(2,1)}) custom-call(s32[64]{0:T(128)S(1)} %multiply_add_fusion.slot_ref, s32[2]{0:T(128)S(1)} %add_convert_fusion.edge_ref, bf16[32,128,128]{2,1,0:T(8,128)(2,1)} %bitcast.21, ...), custom_call_target="tpu_custom_call" | custom-call | flops 38000001024 | bytes 1000000 | tf_op jit(solution)/shard_map/pallas_call | solution.py:336
  266.3 3.4 collective-permute-start.2
  276.3 5.4 %all-to-all-done.4.three_ref = bf16[32,384,128]{2,1,0:T(8,128)(2,1)} async-done(((bf16[32,384,128]{2,1,0:T(8,128)(2,1)}), bf16[32,384,128]{2,1,0:T(8,128)(2,1)}, u32[]{:S(2)}, u32[]{:S(2)}) %all-to-all-start.4) | async-done | bytes 3145760 | tf_op jit(solution)/shard_map/all_to_all | solution.py:348
  281.7 58.0 %all_to_all.35.two_ref = bf16[32,272,128]{2,1,0:T(8,128)(2,1)S(1)} all-to-all(bf16[32,272,128]{2,1,0:T(8,128)(2,1)} %get-tuple-element.86), channel_id=1, replica_groups=mesh['seq'=32,'head'=8] {'seq'}, dimensions={0} | all-to-all | bytes 4456448 | tf_op jit(solution)/shard_map/all_to_all | solution.py:348
  340.5 5.8 %all-to-all-start.6 = ((bf16[32,144,128]{2,1,0:T(8,128)(2,1)}), bf16[32,144,128]{2,1,0:T(8,128)(2,1)S(1)}, u32[]{:S(2)}, u32[]{:S(2)}) async-start(bf16[32,144,128]{2,1,0:T(8,128)(2,1)} %broadcast_dynamic-update-slice_fusion), calls=%async_computation.6 | async-start | bytes 2359296 | tf_op jit(solution)/shard_map/all_to_all | solution.py:348
  346.3 5.7 %shard_map.93 = (bf16[32,128,128]{2,1,0:T(8,128)(2,1)}, bf16[32,128,128]{2,1,0:T(8,128)(2,1)}) custom-call(bf16[32,128,128]{2,1,0:T(8,128)(2,1)} %get-tuple-element.87.od0_ref, bf16[32,128,128]{2,1,0:T(8,128)(2,1)} %get-tuple-element.88.od1_ref), custom_call_target="tpu_custom_call" | custom-call | flops 4000000000 | bytes 1000000 | tf_op jit(solution)/shard_map/pallas_call | solution.py:336
  352.0 5.3 %shard_map.96 = (bf16[32,128,128]{2,1,0:T(8,128)(2,1)}, f32[128,128]{1,0:T(8,128)}) custom-call(s32[96]{0:T(128)S(1)} %reshape.192.wanted_ref, f32[34,128,128]{2,1,0:T(8,128)} %get-tuple-element.97.acc_ref, f32[4096,128]{1,0:T(8,128)} %get-tuple-element.98.far_ref, bf16[2,128,128]{2,1,0:T(8,128)(2,1)S(1)} %collective-permute-done.2.left_ref, ...), custom_call_target="tpu_custom_call" | custom-call | flops 6000000000 | bytes 1000000 | tf_op jit(solution)/shard_map/pallas_call | solution.py:336
  357.3 5.1 %shard_map.95.part_ref = f32[32,128,128]{2,1,0:T(8,128)} custom-call(s32[96]{0:T(128)S(1)} %reshape.192.wanted_ref, f32[34,128,128]{2,1,0:T(8,128)} %get-tuple-element.93.acc_ref, f32[4096,128]{1,0:T(8,128)} %get-tuple-element.94.far_ref, bf16[2,128,128]{2,1,0:T(8,128)(2,1)S(1)} %collective-permute-done.2.left_ref, ...), custom_call_target="tpu_custom_call" | custom-call | flops 4000000000 | bytes 1000000 | tf_op jit(solution)/shard_map/pallas_call | solution.py:336
  362.4 12.2 %all-to-all-done.6.one_ref = bf16[32,144,128]{2,1,0:T(8,128)(2,1)S(1)} async-done(((bf16[32,144,128]{2,1,0:T(8,128)(2,1)}), bf16[32,144,128]{2,1,0:T(8,128)(2,1)S(1)}, u32[]{:S(2)}, u32[]{:S(2)}) %all-to-all-start.6) | async-done | bytes 1179680 | tf_op jit(solution)/shard_map/all_to_all | solution.py:348
  376.1 5.5 %shard_map.97 = (bf16[32,128,128]{2,1,0:T(8,128)(2,1)}, bf16[32,128,128]{2,1,0:T(8,128)(2,1)}) custom-call(s32[96]{0:T(128)S(1)} %reshape.192.wanted_ref, s32[2]{0:T(128)S(1)} %add_convert_fusion.edge_ref, f32[32,128,128]{2,1,0:T(8,128)} %shard_map.95.part_ref, bf16[32,144,128]{2,1,0:T(8,128)(2,1)S(1)} %all-to-all-done.6.one_ref, ...), custom_call_target="tpu_custom_call" | custom-call | flops 4000000000 | bytes 1000000 | tf_op jit(solution)/shard_map/pallas_call | solution.py:336
  (40 shorter events, 23.6 us)
Async XLA Ops:
  3.6 24.4 %all-to-all-start = ((bf16[32,32,128]{2,1,0:T(8,128)(2,1)}), bf16[32,32,128]{2,1,0:T(8,128)(2,1)S(1)}, u32[]{:S(2)}, u32[]{:S(2)}) async-start(bf16[32,32,128]{2,1,0:T(8,128)(2,1)} %get-tuple-element.62), calls=%async_computation | async-start | bytes 524288 | tf_op jit(solution)/shard_map/all_to_all | solution.py:348
  15.3 15.4 %collective-permute-start = (bf16[2,128,128]{2,1,0:T(8,128)(2,1)}, bf16[2,128,128]{2,1,0:T(8,128)(2,1)S(1)}, u32[]{:S(2)}, u32[]{:S(2)}) collective-permute-start(bf16[2,128,128]{2,1,0:T(8,128)(2,1)} %get-tuple-element.64), channel_id=1, source_target_pairs={{0,8},{8,16},{16,24},{24,32},{32,40},{40,48},{48,56},{56,64},{64,7... | collective-permute-start | bytes 196616 | tf_op jit(solution)/shard_map/ppermute | solution.py:394
  18.6 12.0 %collective-permute-start.1 = (bf16[2,128,128]{2,1,0:T(8,128)(2,1)}, bf16[2,128,128]{2,1,0:T(8,128)(2,1)S(1)}, u32[]{:S(2)}, u32[]{:S(2)}) collective-permute-start(bf16[2,128,128]{2,1,0:T(8,128)(2,1)} %get-tuple-element.65), channel_id=1, source_target_pairs={{8,0},{16,8},{24,16},{32,24},{40,32},{48,40},{56,48},{64,56},{72,6... | collective-permute-start | bytes 196616 | tf_op jit(solution)/shard_map/ppermute | solution.py:395
  30.7 40.1 %all-to-all-start.1 = ((bf16[32,144,128]{2,1,0:T(8,128)(2,1)}), bf16[32,144,128]{2,1,0:T(8,128)(2,1)S(1)}, u32[]{:S(2)}, u32[]{:S(2)}) async-start(bf16[32,144,128]{2,1,0:T(8,128)(2,1)} %shard_map.86), calls=%async_computation.1 | async-start | bytes 2359296 | tf_op jit(solution)/shard_map/all_to_all | solution.py:348
  70.7 54.9 %all-to-all-start.2 = ((bf16[32,256,128]{2,1,0:T(8,128)(2,1)}), bf16[32,256,128]{2,1,0:T(8,128)(2,1)S(1)}, u32[]{:S(2)}, u32[]{:S(2)}) async-start(bf16[32,256,128]{2,1,0:T(8,128)(2,1)} %shard_map.87), calls=%async_computation.2 | async-start | bytes 4194304 | tf_op jit(solution)/shard_map/all_to_all | solution.py:348
  86.3 0.7 copy-start
  125.6 1.4 copy-start.2
  127.0 77.9 %all-to-all-start.3 = ((bf16[32,400,128]{2,1,0:T(8,128)(2,1)}), bf16[32,400,128]{2,1,0:T(8,128)(2,1)}, u32[]{:S(2)}, u32[]{:S(2)}) async-start(bf16[32,400,128]{2,1,0:T(8,128)(2,1)} %shard_map.89), calls=%async_computation.3 | async-start | bytes 6553600 | tf_op jit(solution)/shard_map/all_to_all | solution.py:348
  204.9 76.8 %all-to-all-start.4 = ((bf16[32,384,128]{2,1,0:T(8,128)(2,1)}), bf16[32,384,128]{2,1,0:T(8,128)(2,1)}, u32[]{:S(2)}, u32[]{:S(2)}) async-start(bf16[32,384,128]{2,1,0:T(8,128)(2,1)} %get-tuple-element.83), calls=%async_computation.4 | async-start | bytes 6291456 | tf_op jit(solution)/shard_map/all_to_all | solution.py:348
  222.9 42.6 %copy-start.3 = (bf16[2,128,128]{2,1,0:T(8,128)(2,1)S(1)}, bf16[2,128,128]{2,1,0:T(8,128)(2,1)}, u32[]{:S(2)}) copy-start(bf16[2,128,128]{2,1,0:T(8,128)(2,1)} %get-tuple-element.84) | copy-start | bytes 196612
  266.3 7.2 %collective-permute-start.2 = (bf16[2,128,128]{2,1,0:T(8,128)(2,1)S(1)}, bf16[2,128,128]{2,1,0:T(8,128)(2,1)S(1)}, u32[]{:S(2)}, u32[]{:S(2)}) collective-permute-start(bf16[2,128,128]{2,1,0:T(8,128)(2,1)S(1)} %pad_maximum_fusion), channel_id=1, source_target_pairs={{0,8},{8,16},{16,24},{24,32},{32,40},{40,48},{48,56},{56,64},{64,7... | collective-permute-start | bytes 196616 | tf_op jit(solution)/shard_map/ppermute | solution.py:487
  269.7 6.6 %collective-permute-start.3 = (bf16[2,128,128]{2,1,0:T(8,128)(2,1)S(1)}, bf16[2,128,128]{2,1,0:T(8,128)(2,1)S(1)}, u32[]{:S(2)}, u32[]{:S(2)}) collective-permute-start(bf16[2,128,128]{2,1,0:T(8,128)(2,1)S(1)} %pad_maximum_fusion.1), channel_id=1, source_target_pairs={{8,0},{16,8},{24,16},{32,24},{40,32},{48,40},{56,48},{64,56},{72,6... | collective-permute-start | bytes 196616 | tf_op jit(solution)/shard_map/ppermute | solution.py:488
  339.7 12.3 %copy-start.1 = (bf16[32,272,128]{2,1,0:T(8,128)(2,1)}, bf16[32,272,128]{2,1,0:T(8,128)(2,1)S(1)}, u32[]{:S(2)}) copy-start(bf16[32,272,128]{2,1,0:T(8,128)(2,1)S(1)} %all_to_all.35.two_ref) | copy-start | bytes 6684676
  340.5 34.1 %all-to-all-start.6 = ((bf16[32,144,128]{2,1,0:T(8,128)(2,1)}), bf16[32,144,128]{2,1,0:T(8,128)(2,1)S(1)}, u32[]{:S(2)}, u32[]{:S(2)}) async-start(bf16[32,144,128]{2,1,0:T(8,128)(2,1)} %broadcast_dynamic-update-slice_fusion), calls=%async_computation.6 | async-start | bytes 2359296 | tf_op jit(solution)/shard_map/all_to_all | solution.py:348

commit v2 on v1

v2 whole, which is shorter than its diff:
```python
import functools
import math

import jax
import jax.numpy as jnp
from jax import lax
from jax.experimental import pallas as pl
from jax.experimental.pallas import tpu as pltpu
from jax.sharding import PartitionSpec as P

HEAD_DIM = 64
BLOCK = 128
CAP = 3
LATE = BLOCK
LOG2E = math.log2(math.e)
SCALE = HEAD_DIM**-0.5
F32 = jnp.float32
BF16 = jnp.bfloat16
VMEM_LIMIT = 28 * 1024 * 1024

in_vmem = pl.BlockSpec(memory_space=pltpu.VMEM)
in_smem = pl.BlockSpec(memory_space=pltpu.SMEM)


def params():
    return pltpu.CompilerParams(vmem_limit_bytes=VMEM_LIMIT)


def dot(a, b, a_dim, b_dim):
    return lax.dot_general(a, b, (((a_dim,), (b_dim,)), ((), ())), preferred_element_type=F32)


def low_lanes(shape):
    return lax.broadcasted_iota(jnp.int32, shape, len(shape) - 1) < HEAD_DIM


def join(a, b):
    a, b = a.astype(F32), b.astype(F32)
    low = low_lanes(a.shape)
    axis = a.ndim - 1
    first = jnp.where(low, a, pltpu.roll(b, HEAD_DIM, axis))
    second = jnp.where(low, pltpu.roll(a, HEAD_DIM, axis), b)
    return first.astype(BF16), second.astype(BF16)


def pack_kernel(a_ref, b_ref, head0_ref, head1_ref):
    head0_ref[...], head1_ref[...] = join(a_ref[...], b_ref[...])


def ask_kernel(asked_ref, q_ref, k_ref, v_ref, g_ref, k_end_ref, v_end_ref, out_ref, up_ref, down_ref):
    extra = 4 * BLOCK // out_ref.shape[0]
    raw = jnp.concatenate([q_ref[...], k_ref[...], v_ref[...], g_ref[...]], axis=0)
    out_ref[:, :extra] = raw.reshape(out_ref.shape[0], extra, BLOCK)
    out_ref[:, extra:] = asked_ref[...]
    up_ref[0], up_ref[1] = k_end_ref[...], v_end_ref[...]
    down_ref[0], down_ref[1] = k_ref[...], v_ref[...]


def gather_kernel(wanted_ref, kv_ref, *refs):
    out_ref = refs[-1]

    def copy(d, _):
        for r in range(CAP):
            out_ref[d, r * BLOCK : (r + 1) * BLOCK] = kv_ref[wanted_ref[CAP * d + r]]
        for piece_ref in refs[:-1]:
            out_ref[d, CAP * BLOCK :] = piece_ref[...]
        return 0

    lax.fori_loop(0, out_ref.shape[0], copy, 0, unroll=2)


def query_pair(qg):
    low = low_lanes(qg.shape)
    return jnp.concatenate(
        [jnp.where(low, qg * SCALE, 0.0).astype(BF16), jnp.where(low, 0.0, qg).astype(BF16)], axis=0
    )


def main0_kernel(
    slot_ref, edge_ref, qg_ref, kv_ref, low_ref, high_ref, three_ref, raw_ref, stats_ref,
    od_ref, back_ref, acc_ref, side_ref, col_ref, pad_ref, ret_ref,
):
    attend(
        0, slot_ref, edge_ref, qg_ref, kv_ref, low_ref, high_ref, three_ref, raw_ref,
        od_ref, ret_ref, acc_ref, side_ref, col_ref, pad_ref,
    )

    def collect(d, _):
        for r in range(CAP):
            back_ref[d, r * BLOCK : (r + 1) * BLOCK] = ret_ref[CAP * d + r]
        back_ref[d, CAP * BLOCK :] = stats_ref[...]
        return 0

    lax.fori_loop(0, back_ref.shape[0], collect, 0)


def main1_kernel(
    slot_ref, edge_ref, qg_ref, kv_ref, low_ref, high_ref, three_ref, raw_ref, col0_ref,
    od_ref, back_ref, late_ref, acc_ref, side_ref, pad_ref, ret_ref, col_ref,
):
    shards, early = back_ref.shape[0], CAP * BLOCK - LATE
    half, extra = shards // 2, back_ref.shape[1] - early
    attend(
        1, slot_ref, edge_ref, qg_ref, kv_ref, low_ref, high_ref, three_ref, raw_ref,
        od_ref, ret_ref, acc_ref, side_ref, col_ref, pad_ref,
    )

    def collect(d, _):
        back_ref[d, :BLOCK] = ret_ref[CAP * d]
        back_ref[d, BLOCK : 2 * BLOCK] = ret_ref[CAP * d + 1]
        late_ref[d, :LATE] = ret_ref[CAP * d + 2]
        return 0

    lax.fori_loop(0, shards, collect, 0)
    parts = jnp.concatenate([col0_ref[...].astype(BF16), col_ref[...].astype(BF16)], axis=0)
    back_ref[:half, early:] = jnp.zeros((half, extra, BLOCK), BF16)
    back_ref[half:, early:] = parts.reshape(half, extra, BLOCK)
    late_ref[:, LATE:] = jnp.zeros((shards, extra, BLOCK), BF16)


def attend(
    head, slot_ref, edge_ref, qg_ref, kv_ref, low_ref, high_ref, far_ref, raw_ref,
    od_ref, ret_ref, acc_ref, side_ref, col_ref, pad_ref,
):
    blocks = qg_ref.shape[0]
    is_first, is_last = edge_ref[0], edge_ref[1]
    first = join(raw_ref[BLOCK : 2 * BLOCK], raw_ref[2 * BLOCK : 3 * BLOCK])[head]
    pad_ref[0] = join(low_ref[0], low_ref[1])[head]
    pad_ref[blocks + 1] = join(high_ref[0], high_ref[1])[head]
    pad_ref[1 : blocks + 1] = kv_ref[...]
    acc_ref[...] = jnp.zeros_like(acc_ref)
    ret_ref[...] = jnp.zeros_like(ret_ref)
    col_ref[...] = jnp.zeros_like(col_ref)

    def step(j, _):
        slot0, slot1 = slot_ref[2 * j], slot_ref[2 * j + 1]
        keep = 1.0 - ((j == 0) & (is_first == 1)).astype(F32)
        qg = qg_ref[j].astype(F32) * keep
        pair = query_pair(qg)
        window = pad_ref[pl.ds(j, 3)].reshape(3 * BLOCK, BLOCK)
        far0 = far_ref[slot0 // CAP, pl.ds(pl.multiple_of(slot0 % CAP * BLOCK, BLOCK), BLOCK)]
        far1 = far_ref[slot1 // CAP, pl.ds(pl.multiple_of(slot1 % CAP * BLOCK, BLOCK), BLOCK)]
        kv = jnp.concatenate([window, far0, far1, first], axis=0)
        both = dot(kv, pair, 1, 1)
        scores, gw = both[:, :BLOCK], both[:, BLOCK:]
        drop = (j == blocks - 1) & (is_last == 1)
        bias = jnp.where(drop, -jnp.inf, 0.0).astype(F32)
        scores = jnp.concatenate(
            [scores[: 2 * BLOCK], scores[2 * BLOCK : 3 * BLOCK] + bias, scores[3 * BLOCK :]], axis=0
        )
        peak = jnp.max(scores, axis=0, keepdims=True)
        expo = jnp.exp2((scores - peak) * LOG2E)
        weights = expo * (1.0 / jnp.sum(expo, axis=0, keepdims=True))
        wlow = weights.astype(BF16)
        kvt = kv.T
        out_t = dot(kvt, wlow, 1, 0)
        rounded = out_t.astype(BF16).astype(F32)
        row_dot = jnp.sum((rounded * qg.T)[HEAD_DIM:], axis=0, keepdims=True)
        ds = (weights * (gw - row_dot)).astype(BF16)
        dq_t = dot(kvt, ds, 1, 0)
        od_t = jnp.concatenate([dq_t[:HEAD_DIM] * SCALE, out_t[HEAD_DIM:]], axis=0)
        od_ref[j] = od_t.T.astype(BF16)
        terms = dot(jnp.concatenate([ds, wlow], axis=1), pair, 1, 0)
        acc_ref[pl.ds(j, 3)] += terms[: 3 * BLOCK].reshape(3, BLOCK, BLOCK)
        ret_ref[slot0] = terms[3 * BLOCK : 4 * BLOCK].astype(BF16)
        ret_ref[slot1] = terms[4 * BLOCK : 5 * BLOCK].astype(BF16)
        col_ref[...] += terms[5 * BLOCK :]
        return 0

    lax.fori_loop(0, blocks, step, 0)
    side_ref[0] = acc_ref[0].astype(BF16)
    side_ref[1] = acc_ref[blocks + 1].astype(BF16)


def raw_query(raw_ref):
    return join(raw_ref[:BLOCK], raw_ref[3 * BLOCK :])


def two_parts(x):
    high = x.astype(BF16)
    return high, (x - high.astype(F32)).astype(BF16)


def row_forward_kernel(raw_ref, kv0_ref, kv1_ref, stats_ref, peak_ref, out_ref, grad_ref, *, chunk):
    rows = []
    for h, kv_ref in enumerate((kv0_ref, kv1_ref)):
        qg = raw_query(raw_ref)[h].astype(F32)
        pair = query_pair(qg)

        def step(c, carry, kv_ref=kv_ref, pair=pair):
            peak, total, sums = carry
            kv = kv_ref[pl.ds(pl.multiple_of(c * chunk, chunk), chunk)]
            both = dot(kv, pair, 1, 1)
            scores = both[:, :BLOCK]
            new = jnp.maximum(peak, jnp.max(scores, axis=0, keepdims=True))
            shrink = jnp.exp2((peak - new) * LOG2E)
            expo = jnp.exp2((scores - new) * LOG2E)
            total = total * shrink + jnp.sum(expo, axis=0, keepdims=True)
            parts = [*two_parts(expo), *two_parts(expo * both[:, BLOCK:])]
            got = dot(kv.T, jnp.concatenate(parts, axis=1), 1, 0)
            got = [got[:, i * BLOCK : (i + 1) * BLOCK] for i in range(4)]
            sums = [sums[i] * shrink + got[2 * i] + got[2 * i + 1] for i in range(2)]
            return new, total, sums

        start = (
            jnp.full((1, BLOCK), -jnp.inf, F32),
            jnp.zeros((1, BLOCK), F32),
            [jnp.zeros((BLOCK, BLOCK), F32)] * 2,
        )
        peak, total, sums = lax.fori_loop(0, kv_ref.shape[0] // chunk, step, start)
        point = peak.astype(BF16)
        shift = jnp.exp2((peak - point.astype(F32)) * LOG2E)
        out_ref[h], grad_ref[h] = sums[0] * shift, sums[1] * shift
        row_dot = jnp.sum((sums[0] * shift * qg.T)[HEAD_DIM:], axis=0, keepdims=True)
        rows += [point, *two_parts(total * shift), *two_parts(row_dot)]
        peak_ref[h : h + 1] = point.astype(F32)
    rows = [r.astype(F32) for r in rows] + [jnp.zeros((6, BLOCK), F32)]
    stats_ref[...] = jnp.concatenate(rows, axis=0).astype(BF16)


def merged(all_ref, h):
    row = [all_ref[:, 5 * h + i].astype(F32) for i in range(5)]
    peak = jnp.max(row[0], axis=0, keepdims=True)
    grow = jnp.exp2((row[0] - peak) * LOG2E)
    scale = 1.0 / jnp.sum((row[1] + row[2]) * grow, axis=0, keepdims=True)
    return peak, scale, jnp.sum((row[3] + row[4]) * grow, axis=0, keepdims=True) * scale


def row_kernel(all_ref, peak_ref, out_ref, grad_ref, _, sent_ref):
    parts = []
    for h in range(2):
        peak, scale, row_dot = merged(all_ref, h)
        factor = jnp.exp2((peak_ref[h : h + 1] - peak) * LOG2E) * scale
        sums = out_ref[h] * factor
        dq = (grad_ref[h] * factor - sums * row_dot) * SCALE
        parts.append(jnp.concatenate([dq[:HEAD_DIM], sums[HEAD_DIM:]], axis=0).T.astype(BF16))
    sent_ref[...] = jnp.concatenate(parts, axis=0).reshape(sent_ref.shape)


def row_backward_kernel(raw_ref, kv0_ref, kv1_ref, all_ref, far0_ref, far1_ref, *, chunk):
    for h, (kv_ref, far_ref) in enumerate(((kv0_ref, far0_ref), (kv1_ref, far1_ref))):
        pair = query_pair(raw_query(raw_ref)[h].astype(F32))
        peak, scale, row_dot = merged(all_ref, h)

        def step(c, _, kv_ref=kv_ref, far_ref=far_ref, pair=pair, peak=peak, scale=scale, row_dot=row_dot):
            rows = pl.ds(pl.multiple_of(c * chunk, chunk), chunk)
            both = dot(kv_ref[rows], pair, 1, 1)
            weights = jnp.exp2((both[:, :BLOCK] - peak) * LOG2E) * scale
            ds = (weights * (both[:, BLOCK:] - row_dot)).astype(BF16)
            far_ref[rows] = dot(jnp.concatenate([ds, weights.astype(BF16)], axis=1), pair, 1, 0)
            return 0

        lax.fori_loop(0, kv_ref.shape[0] // chunk, step, 0)


def add_slots(tot_ref, wanted_ref, three_ref):
    def add(d, _):
        for r in range(CAP):
            tot_ref[wanted_ref[CAP * d + r]] += three_ref[d, r * BLOCK : (r + 1) * BLOCK].astype(F32)
        return 0

    lax.fori_loop(0, three_ref.shape[0], add, 0)


def own_rows(h, tot_ref, acc_ref, far_ref, left_ref, right_ref):
    blocks = tot_ref.shape[0]
    tot_ref[...] = acc_ref[1 : blocks + 1] + far_ref[...].reshape(tot_ref.shape)
    tot_ref[blocks - 1] += right_ref[h].astype(F32)
    tot_ref[0] += left_ref[h].astype(F32)


def total0_kernel(
    wanted_ref, acc_ref, far_ref, left_ref, right_ref, three_ref, out_ref, block_ref, tot_ref
):
    own_rows(0, tot_ref, acc_ref, far_ref, left_ref, right_ref)
    add_slots(tot_ref, wanted_ref, three_ref)
    block_ref[...] = tot_ref[0]
    out_ref[...] = tot_ref[...].astype(BF16)


def sum_kernel(parts_ref, _, out_ref):
    total = jnp.sum(parts_ref[...].astype(F32), axis=0, keepdims=True).astype(BF16)
    out_ref[...] = jnp.broadcast_to(total, out_ref.shape)


def total1_kernel(wanted_ref, acc_ref, far_ref, left_ref, right_ref, back_ref, tot_ref):
    own_rows(1, tot_ref, acc_ref, far_ref, left_ref, right_ref)

    def add(d, _):
        for r in range(CAP - 1):
            got = back_ref[d, r * BLOCK : (r + 1) * BLOCK]
            tot_ref[wanted_ref[CAP * d + r]] += got.astype(F32)
        return 0

    lax.fori_loop(0, back_ref.shape[0], add, 0)


def last_kernel(
    wanted_ref, edge_ref, part_ref, late_ref, head0_ref, block_ref, att_ref, dq_ref,
    dk_ref, dv_ref, att_out, dq_out, add_ref,
):
    step, count = pl.program_id(0), dk_ref.shape[0]

    @pl.when(step == 0)
    def _():
        add_ref[...] = jnp.zeros_like(add_ref)

        def add(d, _):
            add_ref[wanted_ref[CAP * d + CAP - 1]] += late_ref[d, :LATE].astype(F32)
            return 0

        lax.fori_loop(0, late_ref.shape[0], add, 0)
        is_first = edge_ref[0] == 1
        root = late_ref[:, LATE:].reshape(4 * BLOCK, BLOCK).astype(F32)
        root = [root[i * BLOCK : (i + 1) * BLOCK] for i in range(4)]
        add_ref[0] += root[3] * edge_ref[0].astype(F32)
        dk_ref[0], dv_ref[0] = join(
            block_ref[...] + root[2] * edge_ref[0].astype(F32), part_ref[0] + add_ref[0]
        )
        for new, old_ref, out_ref in zip(join(root[0], root[1]), (dq_ref, att_ref), (dq_out, att_out)):
            out_ref[...] = jnp.where(is_first, new.astype(F32), old_ref[...].astype(F32)).astype(BF16)

    for b in range(count):
        at = step * count + b

        @pl.when(at > 0)
        def _(b=b, at=at):
            dk_ref[b], dv_ref[b] = join(head0_ref[b], part_ref[b] + add_ref[at])


def unpack_kernel(od0_ref, od1_ref, att_ref, dq_ref):
    def write(b, _):
        dq_ref[b], att_ref[b] = join(od0_ref[b], od1_ref[b])
        return 0

    lax.fori_loop(0, od0_ref.shape[0], write, 0)


def in_hbm(x):
    return pltpu.with_memory_space_constraint(x, pltpu.HBM)


def call(kernel, outs, operands, smem=0, scratch=(), us=2, loose=(), free=False):
    return pl.pallas_call(
        kernel,
        out_shape=[jax.ShapeDtypeStruct(s, d) if free else pltpu.HBM(s, d) for s, d in outs],
        in_specs=[in_smem] * smem + [in_vmem] * (len(operands) - smem),
        out_specs=[in_vmem] * len(outs),
        scratch_shapes=[pltpu.VMEM(s, d) for s, d in scratch],
        compiler_params=params(),
        cost_estimate=pl.CostEstimate(flops=us * 10**9, transcendentals=0, bytes_accessed=10**6),
    )(*(x if i < smem or i in loose else in_hbm(x) for i, x in enumerate(operands)))


def exchange(blocks):
    return lax.all_to_all(blocks, "seq", split_axis=0, concat_axis=0, tiled=True)


def after(x, done):
    return lax.optimization_barrier((x, done))


def per_device(query, key, value, grad_out, random_blocks):
    shards, here = lax.axis_size("seq"), lax.axis_index("seq")
    rows = query.shape[0]
    blocks = rows // BLOCK
    slots = shards * CAP
    extra = 4 * BLOCK // shards
    tile = (BLOCK, BLOCK)
    grid = (blocks, *tile)
    forward = [(i, i + 1) for i in range(shards - 1)]
    backward = [(i + 1, i) for i in range(shards - 1)]

    named = random_blocks.reshape(-1)
    owners, inner = named // blocks, named % blocks
    places = jnp.arange(named.shape[0])
    same = (owners[:, None] == owners[None, :]) & (places[None, :] < places[:, None])
    slot_of = owners * CAP + jnp.sum(same.astype(jnp.int32), axis=1)
    asked = jnp.sum(
        jnp.where(slot_of[None, :] == jnp.arange(slots)[:, None], inner[None, :], 0), axis=1
    ).reshape(shards, 1, CAP)
    asked = jnp.pad(asked.astype(BF16), ((0, 0), (0, 15), (0, BLOCK - CAP)))
    top = pl.BlockSpec(tile, lambda i: (0, 0))
    end = pl.BlockSpec(tile, lambda i: (blocks - 1, 0))
    query, key, value, grad_out = (in_hbm(x) for x in (query, key, value, grad_out))
    message, up, down = pl.pallas_call(
        ask_kernel,
        grid=(1,),
        out_shape=[
            pltpu.HBM((shards, extra + 16, BLOCK), BF16),
            pltpu.HBM((2, *tile), BF16),
            pltpu.HBM((2, *tile), BF16),
        ],
        in_specs=[pl.BlockSpec(asked.shape, lambda i: (0, 0, 0)), top, top, top, top, end, end],
        out_specs=[
            pl.BlockSpec((shards, extra + 16, BLOCK), lambda i: (0, 0, 0)),
            pl.BlockSpec((2, *tile), lambda i: (0, 0, 0)),
            pl.BlockSpec((2, *tile), lambda i: (0, 0, 0)),
        ],
        compiler_params=params(),
    )(asked, query, key, value, grad_out, key, value)
    got = exchange(message)
    wanted = got[:, extra, :CAP].astype(jnp.int32).reshape(-1)
    edge = jnp.stack([here == 0, here == shards - 1]).astype(jnp.int32)

    chunk = 512
    part = pl.BlockSpec((chunk, BLOCK), lambda i: (i, 0))

    def pack(a, b):
        return pl.pallas_call(
            pack_kernel,
            grid=(rows // chunk,),
            out_shape=[pltpu.HBM((rows, BLOCK), BF16)] * 2,
            in_specs=[part] * 2,
            out_specs=[part] * 2,
            compiler_params=params(),
        )(a, b)

    kv0, kv1 = pack(key, value)
    steps = 4

    def gather(kv, *pieces):
        (sent,) = call(
            gather_kernel,
            [((shards, CAP * BLOCK + extra * len(pieces), BLOCK), BF16)],
            (wanted, kv.reshape(grid), *pieces),
            smem=1,
            loose=(2,),
        )
        return sent

    three0 = exchange(gather(kv0, got[0, :extra]))
    sent1 = gather(kv1)
    query, grad_out, up, down, sent1 = lax.optimization_barrier((query, grad_out, up, down, sent1))
    qg0, qg1 = pack(in_hbm(query), in_hbm(grad_out))
    low = lax.ppermute(up, "seq", forward)
    high = lax.ppermute(down, "seq", backward)
    sent1, three0, low, high = lax.optimization_barrier((sent1, three0, low, high))
    three1 = exchange(sent1)
    first = three0[:, CAP * BLOCK :].reshape(4 * BLOCK, BLOCK)
    stats, peak, sums, grads = call(
        functools.partial(row_forward_kernel, chunk=chunk),
        [((16, BLOCK), BF16), ((2, BLOCK), F32), ((2, *tile), F32), ((2, *tile), F32)],
        (first, kv0, kv1),
        us=14,
        loose=(0,),
    )
    padded = ((blocks + 2, *tile), BF16)
    returns = ((slots, *tile), BF16)
    od0, back0, acc0, side0, col0 = call(
        main0_kernel,
        [
            (grid, BF16),
            ((shards, CAP * BLOCK + extra, BLOCK), BF16),
            ((blocks + 2, *tile), F32),
            ((2, *tile), BF16),
            (tile, F32),
        ],
        (slot_of, edge, qg0.reshape(grid), kv0.reshape(grid), low, high, three0, first, stats),
        smem=2,
        loose=(4, 5, 6, 7, 8),
        scratch=[padded, returns],
        us=40,
    )
    back0, three1 = after(back0, three1)
    back0 = exchange(back0)
    early = CAP * BLOCK - LATE
    od1, back1, late1, acc1, side1 = call(
        main1_kernel,
        [
            (grid, BF16),
            ((shards, early + extra, BLOCK), BF16),
            ((shards, LATE + extra, BLOCK), BF16),
            ((blocks + 2, *tile), F32),
            ((2, *tile), BF16),
        ],
        (slot_of, edge, qg1.reshape(grid), kv1.reshape(grid), low, high, three1, first, col0),
        smem=2,
        loose=(4, 5, 6, 7),
        scratch=[padded, returns, (tile, F32)],
        us=40,
    )
    left = lax.ppermute(jnp.stack([side0[1], side1[1]]), "seq", forward)
    right = lax.ppermute(jnp.stack([side0[0], side1[0]]), "seq", backward)
    back1, back0, left, right = lax.optimization_barrier((back1, back0, left, right))
    full = lambda shape: pl.BlockSpec(shape, lambda i: (0,) * len(shape))
    behind = pl.BlockSpec((shards, extra, BLOCK), lambda i: (0, CAP * BLOCK // extra, 0))
    ours = pl.BlockSpec((shards // 2, extra, BLOCK), lambda i: (0, early // extra, 0))
    back1 = pl.pallas_call(
        row_kernel,
        grid=(1,),
        out_shape=pltpu.HBM(back1.shape, BF16),
        in_specs=[behind, full((2, BLOCK)), full((2, *tile)), full((2, *tile)), ours],
        out_specs=ours,
        input_output_aliases={4: 0},
        compiler_params=params(),
    )(back0, peak, sums, grads, in_hbm(back1))
    back1 = exchange(back1)
    far0, far1 = pl.pallas_call(
        functools.partial(row_backward_kernel, chunk=chunk),
        grid=(1,),
        out_shape=[pltpu.HBM((rows, BLOCK), F32)] * 2,
        in_specs=[full((4 * BLOCK, BLOCK)), full((rows, BLOCK)), full((rows, BLOCK)), behind],
        out_specs=[full((rows, BLOCK))] * 2,
        compiler_params=params(),
        cost_estimate=pl.CostEstimate(flops=8 * 10**9, transcendentals=0, bytes_accessed=10**6),
    )(first, in_hbm(kv0), in_hbm(kv1), back0)
    attended, grad_query = call(unpack_kernel, [(grid, BF16)] * 2, (od0, od1), us=4)
    whole = [(grid, F32)]
    head0, block0 = call(
        total0_kernel,
        [(grid, BF16), (tile, F32)],
        (wanted, acc0, far0, left, right, back0),
        smem=1,
        scratch=whole,
        us=6,
        loose=(3, 4, 5),
    )
    back1, far1, head0, block0 = lax.optimization_barrier((back1, far1, head0, block0))
    pieces = pl.BlockSpec((shards, extra, BLOCK), lambda i: (0, early // extra, 0))
    tail = pl.BlockSpec((shards, extra, BLOCK), lambda i: (0, LATE // extra, 0))
    late1 = pl.pallas_call(
        sum_kernel,
        grid=(1,),
        out_shape=pltpu.HBM(late1.shape, BF16),
        in_specs=[pieces, pl.BlockSpec((shards, extra, BLOCK), lambda i: (0, LATE // extra, 0))],
        out_specs=tail,
        input_output_aliases={1: 0},
        compiler_params=params(),
    )(back1, in_hbm(late1))
    late1 = exchange(late1)
    (part1,) = call(
        total1_kernel,
        whole,
        (wanted, acc1, far1, left, right, back1),
        smem=1,
        us=4,
        loose=(3, 4, 5),
    )
    out_block = pl.BlockSpec((blocks // steps, *tile), lambda i: (i, 0, 0))
    attended, grad_query = (in_hbm(x.reshape(rows, BLOCK)) for x in (attended, grad_query))
    grad_key, grad_value, attended, grad_query = pl.pallas_call(
        last_kernel,
        grid=(steps,),
        out_shape=[pltpu.HBM(grid, BF16)] * 2 + [pltpu.HBM((rows, BLOCK), BF16)] * 2,
        in_specs=[in_smem, in_smem, out_block, full(late1.shape), out_block, full(tile), top, top],
        out_specs=[out_block, out_block, top, top],
        input_output_aliases={6: 2, 7: 3},
        scratch_shapes=[pltpu.VMEM(grid, F32)],
        compiler_params=params(),
        cost_estimate=pl.CostEstimate(flops=4 * 10**9, transcendentals=0, bytes_accessed=10**6),
    )(wanted, edge, in_hbm(part1), late1, in_hbm(head0), in_hbm(block0), attended, grad_query)
    return attended, grad_query, grad_key.reshape(rows, BLOCK), grad_value.reshape(rows, BLOCK)


def solution(mesh):
    split = P("seq", "head")
    return jax.shard_map(
        per_device,
        mesh=mesh,
        in_specs=(split, split, split, split, P("seq", None)),
        out_specs=(split, split, split, split),
        check_vma=False,
    )
```

time: 383 us -> 379 us (0.990)
  blocking collectives: 58 us -> 0 us
  waiting for transfers between devices: 114 us -> 158 us
  Pallas kernels: 145 us -> 151 us
    all_to_all x1 -> x0, blocking collectives: 58 us -> none  [exchange(): lax.all_to_all(blocks, 'seq', split_axis=0, concat_axis=0, tiled=True)]
    all_to_all x6, waiting for transfers between devices: 110 us -> 149 us  [exchange(): lax.all_to_all(blocks, 'seq', split_axis=0, concat_axis=0, tiled=True)]
    pallas_call x13 -> x14, Pallas kernels: 143 us -> 149 us  [the longest x8 118 us: call(): pl.pallas_call(kernel, out_shape=[jax.ShapeDtypeStruct(s, d) if free else...]
    ppermute x1, waiting for transfers between devices: 0.01 us -> 4.07 us  [per_device(): high = lax.ppermute(down, 'seq', backward)]
  transfers between devices with their start and end apart: 10 -> 10, of which waited for: 7 -> 10; matrix products, arithmetic and copies ran while one was open for 1% -> 0% of each run, Pallas kernels for 36% -> 36%
where the time goes in v2:
time: 379 us; the launch traced here: 378 us
  waiting for transfers between devices  158 us (42%)
  Pallas kernels  151 us (40%)
  starting transfers between devices  60.3 us (16%)
  local copies, waits for them, and re-layouts  6.46 us (2%)
    all_to_all x6, waiting for transfers between devices, exchange(): lax.all_to_all(blocks, 'seq', split_axis=0, concat_axis=0, tiled=True)  149 us
    pallas_call x8, Pallas kernels, call(): pl.pallas_call(kernel, out_shape=[jax.ShapeDtypeStruct(s, d) if free else...  118 us
    all_to_all x6, starting transfers between devices, exchange(): lax.all_to_all(blocks, 'seq', split_axis=0, concat_axis=0, tiled=True)  48.6 us
    pallas_call x2, Pallas kernels, pack(): pl.pallas_call(pack_kernel, grid=(rows // chunk,), out_shape=[pltpu.HBM((...  12.1 us
    pallas_call x1, Pallas kernels, per_device(): pl.pallas_call(functools.partial(row_backward_kernel, chunk=chunk), grid=...  9.99 us
  transfers between devices with their start and end apart: 10, of which 10 were waited for; matrix products, arithmetic and copies ran while one was open for 0% of the time, Pallas kernels for 36%

profile of v2, /device:TPU:2, one launch (start us, length us, event | category | flops | bytes accessed | tf_op | source)
XLA Modules:
  0.0 377.6 jit_solution(10338177290171738216)
XLA Ops:
  3.6 11.6 %all-to-all-start = ((bf16[32,32,128]{2,1,0:T(8,128)(2,1)}), bf16[32,32,128]{2,1,0:T(8,128)(2,1)S(1)}, u32[]{:S(2)}, u32[]{:S(2)}) async-start(bf16[32,32,128]{2,1,0:T(8,128)(2,1)} %get-tuple-element.54), calls=%async_computation | async-start | bytes 524288 | tf_op jit(solution)/shard_map/all_to_all | solution.py:356
  15.2 6.1 %shard_map.85 = (bf16[4096,128]{1,0:T(8,128)(2,1)}, bf16[4096,128]{1,0:T(8,128)(2,1)}) custom-call(bf16[4096,128]{1,0:T(8,128)(2,1)} %a_ref.1, bf16[4096,128]{1,0:T(8,128)(2,1)} %b_ref.1), custom_call_target="tpu_custom_call" | custom-call | tf_op jit(solution)/shard_map/pallas_call | solution.py:410
  21.3 5.1 %all-to-all-done = bf16[32,32,128]{2,1,0:T(8,128)(2,1)S(1)} async-done(((bf16[32,32,128]{2,1,0:T(8,128)(2,1)}), bf16[32,32,128]{2,1,0:T(8,128)(2,1)S(1)}, u32[]{:S(2)}, u32[]{:S(2)}) %all-to-all-start) | async-done | bytes 262176 | tf_op jit(solution)/shard_map/all_to_all | solution.py:356
  29.8 5.6 %all-to-all-start.1 = ((bf16[32,400,128]{2,1,0:T(8,128)(2,1)}), bf16[32,400,128]{2,1,0:T(8,128)(2,1)S(1)}, u32[]{:S(2)}, u32[]{:S(2)}) async-start(bf16[32,400,128]{2,1,0:T(8,128)(2,1)} %shard_map.88), calls=%async_computation.1 | async-start | bytes 6553600 | tf_op jit(solution)/shard_map/all_to_all | solution.py:356
  45.5 4.1 %collective-permute-done.1.high_ref = bf16[2,128,128]{2,1,0:T(8,128)(2,1)S(1)} collective-permute-done((bf16[2,128,128]{2,1,0:T(8,128)(2,1)S(1)}, bf16[2,128,128]{2,1,0:T(8,128)(2,1)S(1)}, u32[]{:S(2)}, u32[]{:S(2)}) %collective-permute-start.1) | collective-permute-done | bytes 65568 | tf_op jit(solution)/shard_map/ppermute | solution.py:437
  49.6 58.8 %all-to-all-done.1.three_ref = bf16[32,400,128]{2,1,0:T(8,128)(2,1)S(1)} async-done(((bf16[32,400,128]{2,1,0:T(8,128)(2,1)}), bf16[32,400,128]{2,1,0:T(8,128)(2,1)S(1)}, u32[]{:S(2)}, u32[]{:S(2)}) %all-to-all-start.1) | async-done | bytes 3276832 | tf_op jit(solution)/shard_map/all_to_all | solution.py:356
  108.4 8.3 %all-to-all-start.2 = ((bf16[32,384,128]{2,1,0:T(8,128)(2,1)}), bf16[32,384,128]{2,1,0:T(8,128)(2,1)}, u32[]{:S(2)}, u32[]{:S(2)}) async-start(bf16[32,384,128]{2,1,0:T(8,128)(2,1)} %shard_map.86), calls=%async_computation.2 | async-start | bytes 6291456 | tf_op jit(solution)/shard_map/all_to_all | solution.py:356
  116.8 6.1 %shard_map.87 = (bf16[4096,128]{1,0:T(8,128)(2,1)}, bf16[4096,128]{1,0:T(8,128)(2,1)}) custom-call(bf16[4096,128]{1,0:T(8,128)(2,1)} %a_ref.2, bf16[4096,128]{1,0:T(8,128)(2,1)} %b_ref.2), custom_call_target="tpu_custom_call" | custom-call | tf_op jit(solution)/shard_map/pallas_call | solution.py:410
  122.9 12.9 %shard_map.89 = (bf16[16,128]{1,0:T(8,128)(2,1)}, f32[2,128]{1,0:T(2,128)}, f32[2,128,128]{2,1,0:T(8,128)}, f32[2,128,128]{2,1,0:T(8,128)}) custom-call(bf16[512,128]{1,0:T(8,128)(2,1)S(1)} %bitcast.13, bf16[4096,128]{1,0:T(8,128)(2,1)} %get-tuple-element.62.kv0_ref, bf16[4096,128]{1,0:T(8,128)(2,1)} %get-tuple-element.57.kv1_ref), custom_call_target="tpu_custom_call" | custom-call | flops 14000000000 | bytes 1000000 | tf_op jit(solution)/shard_map/pallas_call | solution.py:344
  136.5 41.0 %shard_map.90 = (bf16[32,128,128]{2,1,0:T(8,128)(2,1)}, bf16[32,400,128]{2,1,0:T(8,128)(2,1)}, f32[34,128,128]{2,1,0:T(8,128)}, bf16[2,128,128]{2,1,0:T(8,128)(2,1)}, f32[128,128]{1,0:T(8,128)}) custom-call(s32[64]{0:T(128)S(1)} %multiply_add_fusion.slot_ref, s32[2]{0:T(128)S(1)} %add_convert_fusion.edge_ref, bf16[32,128,128]{2,1,0:T(8,128)(2,1)} %bitcast.22, ...), custom_call_target="tpu_custom_call" | custom-call | flops 40000000000 | bytes 1000000 | tf_op jit(solution)/shard_map/pallas_call | solution.py:344
  177.5 10.7 %all-to-all-done.2.three_ref = bf16[32,384,128]{2,1,0:T(8,128)(2,1)} async-done(((bf16[32,384,128]{2,1,0:T(8,128)(2,1)}), bf16[32,384,128]{2,1,0:T(8,128)(2,1)}, u32[]{:S(2)}, u32[]{:S(2)}) %all-to-all-start.2) | async-done | bytes 3145760 | tf_op jit(solution)/shard_map/all_to_all | solution.py:356
  188.2 7.3 %all-to-all-start.3 = ((bf16[32,400,128]{2,1,0:T(8,128)(2,1)}), bf16[32,400,128]{2,1,0:T(8,128)(2,1)S(1)}, u32[]{:S(2)}, u32[]{:S(2)}) async-start(bf16[32,400,128]{2,1,0:T(8,128)(2,1)} %get-tuple-element.76), calls=%async_computation.3 | async-start | bytes 6553600 | tf_op jit(solution)/shard_map/all_to_all | solution.py:356
  198.1 42.2 %shard_map.91 = (bf16[32,128,128]{2,1,0:T(8,128)(2,1)}, bf16[32,272,128]{2,1,0:T(8,128)(2,1)}, bf16[32,144,128]{2,1,0:T(8,128)(2,1)}, f32[34,128,128]{2,1,0:T(8,128)}, bf16[2,128,128]{2,1,0:T(8,128)(2,1)}) custom-call(s32[64]{0:T(128)S(1)} %multiply_add_fusion.slot_ref, s32[2]{0:T(128)S(1)} %add_convert_fusion.edge_ref, bf16[32,128,128]{2,1,0:T(8,128)(2,1)} %bitcast.21, ...), custom_call_target="tpu_custom_call" | custom-call | flops 40000000000 | bytes 1000000 | tf_op jit(solution)/shard_map/pallas_call | solution.py:344
  241.1 3.4 collective-permute-start.2
  252.7 16.5 %all-to-all-done.3.all_ref.three_ref = bf16[32,400,128]{2,1,0:T(8,128)(2,1)S(1)} async-done(((bf16[32,400,128]{2,1,0:T(8,128)(2,1)}), bf16[32,400,128]{2,1,0:T(8,128)(2,1)S(1)}, u32[]{:S(2)}, u32[]{:S(2)}) %all-to-all-start.3) | async-done | bytes 3276832 | tf_op jit(solution)/shard_map/all_to_all | solution.py:356
  271.1 9.4 %all-to-all-start.4 = ((bf16[32,272,128]{2,1,0:T(8,128)(2,1)}), bf16[32,272,128]{2,1,0:T(8,128)(2,1)}, u32[]{:S(2)}, u32[]{:S(2)}) async-start(bf16[32,272,128]{2,1,0:T(8,128)(2,1)} %shard_map.92), calls=%async_computation.4 | async-start | bytes 4456448 | tf_op jit(solution)/shard_map/all_to_all | solution.py:356
  280.5 10.0 %shard_map.93 = (f32[4096,128]{1,0:T(8,128)}, f32[4096,128]{1,0:T(8,128)}) custom-call(bf16[512,128]{1,0:T(8,128)(2,1)S(1)} %bitcast.16, bf16[4096,128]{1,0:T(8,128)(2,1)} %get-tuple-element.62.kv0_ref, bf16[4096,128]{1,0:T(8,128)(2,1)} %get-tuple-element.57.kv1_ref, bf16[32,400,128]{2,1,0:T(8,128)(2,1)S(1)} %all-to-all-done.3.all_ref.three_ref), custom_call_target="tpu_custom_call" | custom-call | flops 8000000000 | bytes 1000000 | tf_op jit(solution)/shard_map/pallas_call | solution.py:499
  290.5 4.4 %shard_map.94 = (bf16[32,128,128]{2,1,0:T(8,128)(2,1)}, f32[128,128]{1,0:T(8,128)}) custom-call(s32[96]{0:T(128)S(1)} %reshape.158.wanted_ref, f32[34,128,128]{2,1,0:T(8,128)} %get-tuple-element.85.acc_ref, f32[4096,128]{1,0:T(8,128)} %get-tuple-element.86.far_ref, bf16[2,128,128]{2,1,0:T(8,128)(2,1)S(1)} %copy-done.11, bf16[2,128,128]{2,1,0:T(8,128)(2,1)S(1)} %copy-done.13, ...), custom_call_target="tpu_custom_call" | custom-call | flops 6000000000 | bytes 1000000 | tf_op jit(solution)/shard_map/pallas_call | solution.py:344
  294.9 37.7 %all-to-all-done.4.back_ref.parts_ref = bf16[32,272,128]{2,1,0:T(8,128)(2,1)} async-done(((bf16[32,272,128]{2,1,0:T(8,128)(2,1)}), bf16[32,272,128]{2,1,0:T(8,128)(2,1)}, u32[]{:S(2)}, u32[]{:S(2)}) %all-to-all-start.4) | async-done | bytes 2228256 | tf_op jit(solution)/shard_map/all_to_all | solution.py:356
  334.3 6.4 %all-to-all-start.5 = ((bf16[32,144,128]{2,1,0:T(8,128)(2,1)}), bf16[32,144,128]{2,1,0:T(8,128)(2,1)S(1)}, u32[]{:S(2)}, u32[]{:S(2)}) async-start(bf16[32,144,128]{2,1,0:T(8,128)(2,1)} %shard_map.96), calls=%async_computation.5 | async-start | bytes 2359296 | tf_op jit(solution)/shard_map/all_to_all | solution.py:356
  340.7 5.7 %shard_map.97 = (bf16[32,128,128]{2,1,0:T(8,128)(2,1)}, bf16[32,128,128]{2,1,0:T(8,128)(2,1)}) custom-call(bf16[32,128,128]{2,1,0:T(8,128)(2,1)} %get-tuple-element.96.od0_ref, bf16[32,128,128]{2,1,0:T(8,128)(2,1)} %get-tuple-element.97.od1_ref), custom_call_target="tpu_custom_call" | custom-call | flops 4000000000 | bytes 1000000 | tf_op jit(solution)/shard_map/pallas_call | solution.py:344
  346.4 5.1 %shard_map.95.part_ref = f32[32,128,128]{2,1,0:T(8,128)} custom-call(s32[96]{0:T(128)S(1)} %reshape.158.wanted_ref, f32[34,128,128]{2,1,0:T(8,128)} %get-tuple-element.74.acc_ref, f32[4096,128]{1,0:T(8,128)} %get-tuple-element.91.far_ref, bf16[2,128,128]{2,1,0:T(8,128)(2,1)S(1)} %copy-done.11, bf16[2,128,128]{2,1,0:T(8,128)(2,1)S(1)} %copy-done.13, ...), custom_call_target="tpu_custom_call" | custom-call | flops 4000000000 | bytes 1000000 | tf_op jit(solution)/shard_map/pallas_call | solution.py:344
  351.5 19.9 %all-to-all-done.5.late_ref = bf16[32,144,128]{2,1,0:T(8,128)(2,1)S(1)} async-done(((bf16[32,144,128]{2,1,0:T(8,128)(2,1)}), bf16[32,144,128]{2,1,0:T(8,128)(2,1)S(1)}, u32[]{:S(2)}, u32[]{:S(2)}) %all-to-all-start.5) | async-done | bytes 1179680 | tf_op jit(solution)/shard_map/all_to_all | solution.py:356
  371.4 6.1 %shard_map.98 = (bf16[32,128,128]{2,1,0:T(8,128)(2,1)}, bf16[32,128,128]{2,1,0:T(8,128)(2,1)}, bf16[4096,128]{1,0:T(8,128)(2,1)}, bf16[4096,128]{1,0:T(8,128)(2,1)}) custom-call(s32[96]{0:T(128)S(1)} %reshape.158.wanted_ref, s32[2]{0:T(128)S(1)} %add_convert_fusion.edge_ref, ...), custom_call_target="tpu_custom_call", output_to_operand_aliasing={{2}: (6, {}), {3}: (7, {})} | custom-call | flops 4000000000 | bytes 1000000 | tf_op jit(solution)/shard_map/pallas_call | solution.py:542
  (64 shorter events, 32.3 us)
Async XLA Ops:
  3.6 22.8 %all-to-all-start = ((bf16[32,32,128]{2,1,0:T(8,128)(2,1)}), bf16[32,32,128]{2,1,0:T(8,128)(2,1)S(1)}, u32[]{:S(2)}, u32[]{:S(2)}) async-start(bf16[32,32,128]{2,1,0:T(8,128)(2,1)} %get-tuple-element.54), calls=%async_computation | async-start | bytes 524288 | tf_op jit(solution)/shard_map/all_to_all | solution.py:356
  29.8 78.5 %all-to-all-start.1 = ((bf16[32,400,128]{2,1,0:T(8,128)(2,1)}), bf16[32,400,128]{2,1,0:T(8,128)(2,1)S(1)}, u32[]{:S(2)}, u32[]{:S(2)}) async-start(bf16[32,400,128]{2,1,0:T(8,128)(2,1)} %shard_map.88), calls=%async_computation.1 | async-start | bytes 6553600 | tf_op jit(solution)/shard_map/all_to_all | solution.py:356
  35.4 3.3 copy-start.17
  35.4 6.6 %copy-start.16 = (bf16[2,128,128]{2,1,0:T(8,128)(2,1)S(1)}, bf16[2,128,128]{2,1,0:T(8,128)(2,1)}, u32[]{:S(2)}) copy-start(bf16[2,128,128]{2,1,0:T(8,128)(2,1)} %get-tuple-element.64) | copy-start | bytes 196612
  38.7 6.8 %collective-permute-start = (bf16[2,128,128]{2,1,0:T(8,128)(2,1)S(1)}, bf16[2,128,128]{2,1,0:T(8,128)(2,1)S(1)}, u32[]{:S(2)}, u32[]{:S(2)}) collective-permute-start(bf16[2,128,128]{2,1,0:T(8,128)(2,1)S(1)} %copy-done.17), channel_id=1, source_target_pairs={{0,8},{8,16},{16,24},{24,32},{32,40},{40,48},{48,56},{56,64},{64,7... | collective-permute-start | bytes 196616 | tf_op jit(solution)/shard_map/ppermute | solution.py:436
  42.1 7.5 %collective-permute-start.1 = (bf16[2,128,128]{2,1,0:T(8,128)(2,1)S(1)}, bf16[2,128,128]{2,1,0:T(8,128)(2,1)S(1)}, u32[]{:S(2)}, u32[]{:S(2)}) collective-permute-start(bf16[2,128,128]{2,1,0:T(8,128)(2,1)S(1)} %copy-done.16), channel_id=1, source_target_pairs={{8,0},{16,8},{24,16},{32,24},{40,32},{48,40},{56,48},{64,56},{72,6... | collective-permute-start | bytes 196616 | tf_op jit(solution)/shard_map/ppermute | solution.py:437
  45.5 90.3 %copy-start.6 = (bf16[2,128,128]{2,1,0:T(8,128)(2,1)}, bf16[2,128,128]{2,1,0:T(8,128)(2,1)S(1)}, u32[]{:S(2)}) copy-start(bf16[2,128,128]{2,1,0:T(8,128)(2,1)S(1)} %collective-permute-done.low_ref) | copy-start | bytes 196612
  49.6 86.2 %copy-start.8 = (bf16[2,128,128]{2,1,0:T(8,128)(2,1)}, bf16[2,128,128]{2,1,0:T(8,128)(2,1)S(1)}, u32[]{:S(2)}) copy-start(bf16[2,128,128]{2,1,0:T(8,128)(2,1)S(1)} %collective-permute-done.1.high_ref) | copy-start | bytes 196612
  108.4 79.8 %all-to-all-start.2 = ((bf16[32,384,128]{2,1,0:T(8,128)(2,1)}), bf16[32,384,128]{2,1,0:T(8,128)(2,1)}, u32[]{:S(2)}, u32[]{:S(2)}) async-start(bf16[32,384,128]{2,1,0:T(8,128)(2,1)} %shard_map.86), calls=%async_computation.2 | async-start | bytes 6291456 | tf_op jit(solution)/shard_map/all_to_all | solution.py:356
  122.9 12.9 %copy-start.2 = (bf16[32,16,128]{2,1,0:T(8,128)(2,1)}, bf16[32,16,128]{2,1,0:T(8,128)(2,1)S(1)}, u32[]{:S(2)}) copy-start(bf16[32,16,128]{2,1,0:T(8,128)(2,1)S(1)} %slice.23) | copy-start | bytes 393220
  188.2 81.1 %all-to-all-start.3 = ((bf16[32,400,128]{2,1,0:T(8,128)(2,1)}), bf16[32,400,128]{2,1,0:T(8,128)(2,1)S(1)}, u32[]{:S(2)}, u32[]{:S(2)}) async-start(bf16[32,400,128]{2,1,0:T(8,128)(2,1)} %get-tuple-element.76), calls=%async_computation.3 | async-start | bytes 6553600 | tf_op jit(solution)/shard_map/all_to_all | solution.py:356
  195.5 0.9 copy-start.3
  196.4 0.8 copy-start.7
  198.0 42.2 %copy-start.15 = (bf16[2,128,128]{2,1,0:T(8,128)(2,1)S(1)}, bf16[2,128,128]{2,1,0:T(8,128)(2,1)}, u32[]{:S(2)}) copy-start(bf16[2,128,128]{2,1,0:T(8,128)(2,1)} %get-tuple-element.77) | copy-start | bytes 196612
  198.0 71.2 %copy-start = (f32[2,128,128]{2,1,0:T(8,128)S(1)}, f32[2,128,128]{2,1,0:T(8,128)}, u32[]{:S(2)}) copy-start(f32[2,128,128]{2,1,0:T(8,128)} %get-tuple-element.81.out_ref) | copy-start | bytes 393220
  198.1 71.2 %copy-start.1 = (f32[2,128,128]{2,1,0:T(8,128)S(1)}, f32[2,128,128]{2,1,0:T(8,128)}, u32[]{:S(2)}) copy-start(f32[2,128,128]{2,1,0:T(8,128)} %get-tuple-element.82.grad_ref) | copy-start | bytes 393220
  198.1 71.2 %copy-start.5 = (f32[2,128]{1,0:T(2,128)S(1)}, f32[2,128]{1,0:T(2,128)}, u32[]{:S(2)}) copy-start(f32[2,128]{1,0:T(2,128)} %get-tuple-element.80.peak_ref) | copy-start | bytes 3076
  241.1 8.0 %collective-permute-start.2 = (bf16[2,128,128]{2,1,0:T(8,128)(2,1)S(1)}, bf16[2,128,128]{2,1,0:T(8,128)(2,1)S(1)}, u32[]{:S(2)}, u32[]{:S(2)}) collective-permute-start(bf16[2,128,128]{2,1,0:T(8,128)(2,1)S(1)} %pad_maximum_fusion), channel_id=1, source_target_pairs={{0,8},{8,16},{16,24},{24,32},{32,40},{40,48},{48,56},{56,64},{64,7... | collective-permute-start | bytes 196616 | tf_op jit(solution)/shard_map/ppermute | solution.py:483
  244.5 7.6 %collective-permute-start.3 = (bf16[2,128,128]{2,1,0:T(8,128)(2,1)S(1)}, bf16[2,128,128]{2,1,0:T(8,128)(2,1)S(1)}, u32[]{:S(2)}, u32[]{:S(2)}) collective-permute-start(bf16[2,128,128]{2,1,0:T(8,128)(2,1)S(1)} %pad_maximum_fusion.1), channel_id=1, source_target_pairs={{8,0},{16,8},{24,16},{32,24},{40,32},{48,40},{56,48},{64,56},{72,6... | collective-permute-start | bytes 196616 | tf_op jit(solution)/shard_map/ppermute | solution.py:484
  271.1 9.4 %copy-start.4 = (bf16[32,16,128]{2,1,0:T(8,128)(2,1)S(1)}, bf16[32,16,128]{2,1,0:T(8,128)(2,1)}, u32[]{:S(2)}) copy-start(bf16[32,16,128]{2,1,0:T(8,128)(2,1)} %copy-done.2) | copy-start | bytes 393220
  271.1 61.6 %all-to-all-start.4 = ((bf16[32,272,128]{2,1,0:T(8,128)(2,1)}), bf16[32,272,128]{2,1,0:T(8,128)(2,1)}, u32[]{:S(2)}, u32[]{:S(2)}) async-start(bf16[32,272,128]{2,1,0:T(8,128)(2,1)} %shard_map.92), calls=%async_computation.4 | async-start | bytes 4456448 | tf_op jit(solution)/shard_map/all_to_all | solution.py:356
  280.5 10.0 %copy-start.11 = (bf16[2,128,128]{2,1,0:T(8,128)(2,1)S(1)}, bf16[2,128,128]{2,1,0:T(8,128)(2,1)}, u32[]{:S(2)}) copy-start(bf16[2,128,128]{2,1,0:T(8,128)(2,1)} %copy-done.10) | copy-start | bytes 196612
  280.5 10.0 %copy-start.13 = (bf16[2,128,128]{2,1,0:T(8,128)(2,1)S(1)}, bf16[2,128,128]{2,1,0:T(8,128)(2,1)}, u32[]{:S(2)}) copy-start(bf16[2,128,128]{2,1,0:T(8,128)(2,1)} %copy-done.12) | copy-start | bytes 196612
  334.3 37.1 %all-to-all-start.5 = ((bf16[32,144,128]{2,1,0:T(8,128)(2,1)}), bf16[32,144,128]{2,1,0:T(8,128)(2,1)S(1)}, u32[]{:S(2)}, u32[]{:S(2)}) async-start(bf16[32,144,128]{2,1,0:T(8,128)(2,1)} %shard_map.96), calls=%async_computation.5 | async-start | bytes 2359296 | tf_op jit(solution)/shard_map/all_to_all | solution.py:356
  (4 other events, 2.8 us)

commit v3 on v1

--- a/solution.py
+++ b/solution.py
@@ -15,7 +15,7 @@
 SCALE = HEAD_DIM**-0.5
 F32 = jnp.float32
 BF16 = jnp.bfloat16
-VMEM_LIMIT = 52 * 1024 * 1024
+VMEM_LIMIT = 28 * 1024 * 1024
 
 in_vmem = pl.BlockSpec(memory_space=pltpu.VMEM)
 in_smem = pl.BlockSpec(memory_space=pltpu.SMEM)
@@ -42,9 +42,8 @@
     return first.astype(BF16), second.astype(BF16)
 
 
-def pack_kernel(q_ref, k_ref, v_ref, g_ref, qg0_ref, qg1_ref, kv0_ref, kv1_ref):
-    qg0_ref[...], qg1_ref[...] = join(q_ref[...], g_ref[...])
-    kv0_ref[...], kv1_ref[...] = join(k_ref[...], v_ref[...])
+def pack_kernel(a_ref, b_ref, head0_ref, head1_ref):
+    head0_ref[...], head1_ref[...] = join(a_ref[...], b_ref[...])
 
 
 def ask_kernel(asked_ref, q_ref, k_ref, v_ref, g_ref, k_end_ref, v_end_ref, out_ref, up_ref, down_ref):
@@ -57,12 +56,11 @@
 
 
 def gather0_kernel(wanted_ref, kv_ref, piece_ref, out_ref):
-    def copy(d, _):
-        out_ref[d, :BLOCK] = kv_ref[wanted_ref[CAP * d]]
+    count = out_ref.shape[0]
+    start = pl.program_id(0) * count
+    for d in range(count):
+        out_ref[d, :BLOCK] = kv_ref[wanted_ref[CAP * (start + d)]]
         out_ref[d, BLOCK:] = piece_ref[...]
-        return 0
-
-    lax.fori_loop(0, out_ref.shape[0], copy, 0, unroll=2)
 
 
 def gather0_rest_kernel(wanted_ref, kv_ref, out_ref):
@@ -95,13 +93,9 @@
     slot_ref, edge_ref, qg_ref, kv_ref, low_ref, high_ref, one_ref, two_ref, raw_ref,
     od_ref, back_ref, acc_ref, side_ref, col_ref, pad_ref, far_ref, ret_ref,
 ):
-    def spread(d, _):
-        far_ref[CAP * d] = one_ref[d, :BLOCK]
-        far_ref[CAP * d + 1] = two_ref[d, :BLOCK]
-        far_ref[CAP * d + 2] = two_ref[d, BLOCK:]
-        return 0
-
-    lax.fori_loop(0, one_ref.shape[0], spread, 0)
+    shards = one_ref.shape[0]
+    far_ref[:, :BLOCK] = one_ref[:, :BLOCK]
+    far_ref[:, BLOCK:] = two_ref[...]
     attend(
         0, slot_ref, edge_ref, qg_ref, kv_ref, low_ref, high_ref, far_ref, raw_ref,
         od_ref, ret_ref, acc_ref, side_ref, col_ref, pad_ref,
@@ -112,23 +106,17 @@
             back_ref[d, r * BLOCK : (r + 1) * BLOCK] = ret_ref[CAP * d + r]
         return 0
 
-    lax.fori_loop(0, one_ref.shape[0], collect, 0)
+    lax.fori_loop(0, shards, collect, 0)
 
 
 def main1_kernel(
     slot_ref, edge_ref, qg_ref, kv_ref, low_ref, high_ref, three_ref, raw_ref, row_ref, col0_ref,
-    od_ref, two_ref, one_ref, acc_ref, side_ref, pad_ref, far_ref, ret_ref, col_ref,
+    od_ref, two_ref, one_ref, acc_ref, side_ref, pad_ref, ret_ref, col_ref,
 ):
     shards, extra = one_ref.shape[0], one_ref.shape[1] - BLOCK
 
-    def spread(d, _):
-        for r in range(CAP):
-            far_ref[CAP * d + r] = three_ref[d, r * BLOCK : (r + 1) * BLOCK]
-        return 0
-
-    lax.fori_loop(0, shards, spread, 0)
     attend(
-        1, slot_ref, edge_ref, qg_ref, kv_ref, low_ref, high_ref, far_ref, raw_ref,
+        1, slot_ref, edge_ref, qg_ref, kv_ref, low_ref, high_ref, three_ref, raw_ref,
         od_ref, ret_ref, acc_ref, side_ref, col_ref, pad_ref,
     )
 
@@ -165,7 +153,9 @@
         qg = qg_ref[j].astype(F32) * keep
         pair = query_pair(qg)
         window = pad_ref[pl.ds(j, 3)].reshape(3 * BLOCK, BLOCK)
-        kv = jnp.concatenate([window, far_ref[slot0], far_ref[slot1], first], axis=0)
+        far0 = far_ref[slot0 // CAP, pl.ds(pl.multiple_of(slot0 % CAP * BLOCK, BLOCK), BLOCK)]
+        far1 = far_ref[slot1 // CAP, pl.ds(pl.multiple_of(slot1 % CAP * BLOCK, BLOCK), BLOCK)]
+        kv = jnp.concatenate([window, far0, far1, first], axis=0)
         both = dot(kv, pair, 1, 1)
         scores, gw = both[:, :BLOCK], both[:, BLOCK:]
         drop = (j == blocks - 1) & (is_last == 1)
@@ -298,19 +288,36 @@
 
 
 def last_kernel(
-    wanted_ref, edge_ref, part_ref, one_ref, head0_ref, block_ref, dk_ref, dv_ref, tot_ref
+    wanted_ref, edge_ref, part_ref, late_ref, head0_ref, block_ref, att_ref, dq_ref,
+    dk_ref, dv_ref, att_out, dq_out, add_ref,
 ):
-    tot_ref[...] = part_ref[...]
-    add_slots(tot_ref, wanted_ref, one_ref, range(2, CAP))
-    root = one_ref[:, BLOCK:].reshape(4 * BLOCK, BLOCK).astype(F32) * edge_ref[0].astype(F32)
-    tot_ref[0] += root[3 * BLOCK :]
-
-    def write(b, _):
-        dk_ref[b], dv_ref[b] = join(head0_ref[b], tot_ref[b])
-        return 0
-
-    lax.fori_loop(0, tot_ref.shape[0], write, 0, unroll=2)
-    dk_ref[0], dv_ref[0] = join(block_ref[...] + root[2 * BLOCK : 3 * BLOCK], tot_ref[0])
+    step, count = pl.program_id(0), dk_ref.shape[0]
+
+    @pl.when(step == 0)
+    def _():
+        add_ref[...] = jnp.zeros_like(add_ref)
+
+        def add(d, _):
+            add_ref[wanted_ref[CAP * d + CAP - 1]] += late_ref[d, :BLOCK].astype(F32)
+            return 0
+
+        lax.fori_loop(0, late_ref.shape[0], add, 0)
+        is_first = edge_ref[0] == 1
+        root = late_ref[:, BLOCK:].reshape(4 * BLOCK, BLOCK).astype(F32)
+        root = [root[i * BLOCK : (i + 1) * BLOCK] for i in range(4)]
+        add_ref[0] += root[3] * edge_ref[0].astype(F32)
+        dk_ref[0], dv_ref[0] = join(
+            block_ref[...] + root[2] * edge_ref[0].astype(F32), part_ref[0] + add_ref[0]
+        )
+        for new, old_ref, out_ref in zip(join(root[0], root[1]), (dq_ref, att_ref), (dq_out, att_out)):
+            out_ref[...] = jnp.where(is_first, new.astype(F32), old_ref[...].astype(F32)).astype(BF16)
+
+    for b in range(count):
+        at = step * count + b
+
+        @pl.when(at > 0)
+        def _(b=b, at=at):
+            dk_ref[b], dv_ref[b] = join(head0_ref[b], part_ref[b] + add_ref[at])
 
 
 def unpack_kernel(od0_ref, od1_ref, att_ref, dq_ref):
@@ -319,13 +326,6 @@
         return 0
 
     lax.fori_loop(0, od0_ref.shape[0], write, 0)
-
-
-def root_kernel(edge_ref, root_ref, att_ref, dq_ref, att_out, dq_out):
-    dq, att = join(root_ref[:BLOCK], root_ref[BLOCK : 2 * BLOCK])
-    is_first = edge_ref[0] == 1
-    att_out[...] = jnp.where(is_first, att.astype(F32), att_ref[...].astype(F32)).astype(BF16)
-    dq_out[...] = jnp.where(is_first, dq.astype(F32), dq_ref[...].astype(F32)).astype(BF16)
 
 
 def in_hbm(x):
@@ -391,38 +391,49 @@
         ],
         compiler_params=params(),
     )(asked, query, key, value, grad_out, key, value)
-    low = lax.ppermute(up, "seq", forward)
-    high = lax.ppermute(down, "seq", backward)
     got = exchange(message)
     wanted = got[:, extra, :CAP].astype(jnp.int32).reshape(-1)
     edge = jnp.stack([here == 0, here == shards - 1]).astype(jnp.int32)
 
     chunk = 512
     part = pl.BlockSpec((chunk, BLOCK), lambda i: (i, 0))
-    qg0, qg1, kv0, kv1 = pl.pallas_call(
-        pack_kernel,
-        grid=(rows // chunk,),
-        out_shape=[pltpu.HBM((rows, BLOCK), BF16)] * 4,
-        in_specs=[part] * 4,
-        out_specs=[part] * 4,
+
+    def pack(a, b):
+        return pl.pallas_call(
+            pack_kernel,
+            grid=(rows // chunk,),
+            out_shape=[pltpu.HBM((rows, BLOCK), BF16)] * 2,
+            in_specs=[part] * 2,
+            out_specs=[part] * 2,
+            compiler_params=params(),
+        )(a, b)
+
+    kv0, kv1 = pack(key, value)
+    steps = 4
+    one0 = pl.pallas_call(
+        gather0_kernel,
+        grid=(steps,),
+        out_shape=pltpu.HBM((shards, BLOCK + extra, BLOCK), BF16),
+        in_specs=[
+            in_smem,
+            pl.BlockSpec(grid, lambda i: (0, 0, 0)),
+            pl.BlockSpec((extra, BLOCK), lambda i: (0, 0)),
+        ],
+        out_specs=pl.BlockSpec((shards // steps, BLOCK + extra, BLOCK), lambda i: (i, 0, 0)),
         compiler_params=params(),
-    )(query, key, value, grad_out)
-    (one0,) = call(
-        gather0_kernel,
-        [((shards, BLOCK + extra, BLOCK), BF16)],
-        (wanted, kv0.reshape(grid), got[0, :extra]),
-        smem=1,
-        loose=(2,),
-    )
+    )(wanted, in_hbm(kv0.reshape(grid)), got[0, :extra])
     (two0,) = call(
         gather0_rest_kernel,
         [((shards, 2 * BLOCK, BLOCK), BF16)],
         (wanted, kv0.reshape(grid)),
         smem=1,
     )
-    one0, low, high = lax.optimization_barrier((one0, low, high))
     one0 = exchange(one0)
-    two0, one0 = after(two0, one0)
+    query, grad_out, up, down, two0 = lax.optimization_barrier((query, grad_out, up, down, two0))
+    qg0, qg1 = pack(in_hbm(query), in_hbm(grad_out))
+    low = lax.ppermute(up, "seq", forward)
+    high = lax.ppermute(down, "seq", backward)
+    two0, one0, low, high = lax.optimization_barrier((two0, one0, low, high))
     two0 = exchange(two0)
     first = one0[:, BLOCK:].reshape(4 * BLOCK, BLOCK)
     stats, peak, partial = call(
@@ -441,7 +452,8 @@
     )
     three1, two0 = after(three1, two0)
     three1 = exchange(three1)
-    scratch = [((blocks + 2, *tile), BF16), ((slots, *tile), BF16), ((slots, *tile), BF16)]
+    padded = ((blocks + 2, *tile), BF16)
+    returns = ((slots, *tile), BF16)
     od0, back0, acc0, side0, col0 = call(
         main0_kernel,
         [
@@ -454,7 +466,7 @@
         (slot_of, edge, qg0.reshape(grid), kv0.reshape(grid), low, high, one0, two0, first),
         smem=2,
         loose=(4, 5, 6, 7, 8),
-        scratch=scratch,
+        scratch=[padded, ((shards, CAP * BLOCK, BLOCK), BF16), returns],
         us=38,
     )
     back0, three1 = after(back0, three1)
@@ -481,7 +493,7 @@
         ),
         smem=2,
         loose=(4, 5, 6, 7),
-        scratch=[*scratch, (tile, F32)],
+        scratch=[padded, returns, (tile, F32)],
         us=38,
     )
     left = lax.ppermute(jnp.stack([side0[1], side1[1]]), "seq", forward)
@@ -498,36 +510,33 @@
         [(grid, BF16), (tile, F32)],
         (wanted, acc0, far0, left, right, back0),
         smem=1,
-        loose=(3, 4, 5),
         scratch=whole,
         us=6,
+        loose=(3, 4, 5),
     )
     (part1,) = call(
-        total1_kernel, whole, (wanted, acc1, far1, left, right, two1), smem=1, us=4, loose=(3, 4, 5)
-    )
-    grad_key, grad_value = call(
+        total1_kernel,
+        whole,
+        (wanted, acc1, far1, left, right, two1),
+        smem=1,
+        us=4,
+        loose=(3, 4, 5),
+    )
+    full = lambda shape: pl.BlockSpec(shape, lambda i: (0,) * len(shape))
+    out_block = pl.BlockSpec((blocks // steps, *tile), lambda i: (i, 0, 0))
+    attended, grad_query = (in_hbm(x.reshape(rows, BLOCK)) for x in (attended, grad_query))
+    grad_key, grad_value, attended, grad_query = pl.pallas_call(
         last_kernel,
-        [(grid, BF16)] * 2,
-        (wanted, edge, part1, one1, head0, block0),
-        smem=2,
-        loose=(3,),
-        scratch=whole,
-        us=4,
-    )
-    attended, grad_query, grad_key, grad_value = (
-        x.reshape(rows, BLOCK) for x in (attended, grad_query, grad_key, grad_value)
-    )
-    root = one1[:, BLOCK:].reshape(4 * BLOCK, BLOCK)
-    attended, grad_query = pl.pallas_call(
-        root_kernel,
-        grid=(1,),
-        out_shape=[pltpu.HBM((rows, BLOCK), BF16)] * 2,
-        in_specs=[in_smem, pl.BlockSpec((4 * BLOCK, BLOCK), lambda i: (0, 0)), top, top],
-        out_specs=[top, top],
-        input_output_aliases={2: 0, 3: 1},
+        grid=(steps,),
+        out_shape=[pltpu.HBM(grid, BF16)] * 2 + [pltpu.HBM((rows, BLOCK), BF16)] * 2,
+        in_specs=[in_smem, in_smem, out_block, full(one1.shape), out_block, full(tile), top, top],
+        out_specs=[out_block, out_block, top, top],
+        input_output_aliases={6: 2, 7: 3},
+        scratch_shapes=[pltpu.VMEM(grid, F32)],
         compiler_params=params(),
-    )(edge, root, in_hbm(attended), in_hbm(grad_query))
-    return attended, grad_query, grad_key, grad_value
+        cost_estimate=pl.CostEstimate(flops=4 * 10**9, transcendentals=0, bytes_accessed=10**6),
+    )(wanted, edge, in_hbm(part1), one1, in_hbm(head0), in_hbm(block0), attended, grad_query)
+    return attended, grad_query, grad_key.reshape(rows, BLOCK), grad_value.reshape(rows, BLOCK)
 
 
 def solution(mesh):

time: 383 us -> 374 us (0.977)
  waiting for transfers between devices: 114 us -> 108 us
  starting transfers between devices: 58 us -> 53.1 us
    pallas_call x2 -> x4, Pallas kernels: 8.44 us -> 21.3 us  [the longest x2 12.3 us: pack(): pl.pallas_call(pack_kernel, grid=(rows // chunk,), out_shape=[pltpu.HBM((...]
    all_to_all x6, waiting for transfers between devices: 110 us -> 97.8 us  [exchange(): lax.all_to_all(blocks, 'seq', split_axis=0, concat_axis=0, tiled=True)]
    pallas_call x11 -> x9, Pallas kernels: 135 us -> 124 us  [call(): pl.pallas_call(kernel, out_shape=[pltpu.HBM(s, d) for s, d in outs], in_s...]
    all_to_all x6, starting transfers between devices: 46.3 us -> 41.5 us  [exchange(): lax.all_to_all(blocks, 'seq', split_axis=0, concat_axis=0, tiled=True)]
    ppermute x1, waiting for transfers between devices: 0.01 us -> 3.97 us  [per_device(): high = lax.ppermute(down, 'seq', backward)]
  transfers between devices with their start and end apart: 10 -> 10, of which waited for: 7 -> 10; matrix products, arithmetic and copies ran while one was open for 1% -> 0% of each run, Pallas kernels for 36% -> 37%
where the time goes in v3:
time: 374 us; the launch traced here: 372 us
  Pallas kernels  147 us (39%)
  waiting for transfers between devices  108 us (29%)
  blocking collectives  57 us (15%)
  starting transfers between devices  53.1 us (14%)
  local copies, waits for them, and re-layouts  5.94 us (2%)
    pallas_call x9, Pallas kernels, call(): pl.pallas_call(kernel, out_shape=[pltpu.HBM(s, d) for s, d in outs], in_s...  124 us
    all_to_all x6, waiting for transfers between devices, exchange(): lax.all_to_all(blocks, 'seq', split_axis=0, concat_axis=0, tiled=True)  97.8 us
    all_to_all x1, blocking collectives, exchange(): lax.all_to_all(blocks, 'seq', split_axis=0, concat_axis=0, tiled=True)  57 us
    all_to_all x6, starting transfers between devices, exchange(): lax.all_to_all(blocks, 'seq', split_axis=0, concat_axis=0, tiled=True)  41.5 us
    pallas_call x2, Pallas kernels, pack(): pl.pallas_call(pack_kernel, grid=(rows // chunk,), out_shape=[pltpu.HBM((...  12.3 us
  transfers between devices with their start and end apart: 10, of which 10 were waited for; matrix products, arithmetic and copies ran while one was open for 0% of the time, Pallas kernels for 37%

profile of v3, /device:TPU:2, one launch (start us, length us, event | category | flops | bytes accessed | tf_op | source)
XLA Modules:
  0.0 372.4 jit_solution(10449439243622259937)
XLA Ops:
  3.6 11.6 %all-to-all-start = ((bf16[32,32,128]{2,1,0:T(8,128)(2,1)}), bf16[32,32,128]{2,1,0:T(8,128)(2,1)S(1)}, u32[]{:S(2)}, u32[]{:S(2)}) async-start(bf16[32,32,128]{2,1,0:T(8,128)(2,1)} %get-tuple-element.64), calls=%async_computation | async-start | bytes 524288 | tf_op jit(solution)/shard_map/all_to_all | solution.py:348
  15.2 6.1 %shard_map.85 = (bf16[4096,128]{1,0:T(8,128)(2,1)}, bf16[4096,128]{1,0:T(8,128)(2,1)}) custom-call(bf16[4096,128]{1,0:T(8,128)(2,1)} %a_ref.1, bf16[4096,128]{1,0:T(8,128)(2,1)} %b_ref.1), custom_call_target="tpu_custom_call" | custom-call | tf_op jit(solution)/shard_map/pallas_call | solution.py:402
  21.3 5.1 %all-to-all-done = bf16[32,32,128]{2,1,0:T(8,128)(2,1)S(1)} async-done(((bf16[32,32,128]{2,1,0:T(8,128)(2,1)}), bf16[32,32,128]{2,1,0:T(8,128)(2,1)S(1)}, u32[]{:S(2)}, u32[]{:S(2)}) %all-to-all-start) | async-done | bytes 262176 | tf_op jit(solution)/shard_map/all_to_all | solution.py:348
  29.5 5.6 %all-to-all-start.1 = ((bf16[32,144,128]{2,1,0:T(8,128)(2,1)}), bf16[32,144,128]{2,1,0:T(8,128)(2,1)S(1)}, u32[]{:S(2)}, u32[]{:S(2)}) async-start(bf16[32,144,128]{2,1,0:T(8,128)(2,1)} %shard_map.88), calls=%async_computation.1 | async-start | bytes 2359296 | tf_op jit(solution)/shard_map/all_to_all | solution.py:348
  44.2 4.0 %collective-permute-done.1.high_ref = bf16[2,128,128]{2,1,0:T(8,128)(2,1)S(1)} collective-permute-done((bf16[2,128,128]{2,1,0:T(8,128)(2,1)S(1)}, bf16[2,128,128]{2,1,0:T(8,128)(2,1)S(1)}, u32[]{:S(2)}, u32[]{:S(2)}) %collective-permute-start.1) | collective-permute-done | bytes 65568 | tf_op jit(solution)/shard_map/ppermute | solution.py:435
  48.1 17.0 %all-to-all-done.1.one_ref = bf16[32,144,128]{2,1,0:T(8,128)(2,1)S(1)} async-done(((bf16[32,144,128]{2,1,0:T(8,128)(2,1)}), bf16[32,144,128]{2,1,0:T(8,128)(2,1)S(1)}, u32[]{:S(2)}, u32[]{:S(2)}) %all-to-all-start.1) | async-done | bytes 1179680 | tf_op jit(solution)/shard_map/all_to_all | solution.py:348
  65.1 6.3 %all-to-all-start.2 = ((bf16[32,256,128]{2,1,0:T(8,128)(2,1)}), bf16[32,256,128]{2,1,0:T(8,128)(2,1)S(1)}, u32[]{:S(2)}, u32[]{:S(2)}) async-start(bf16[32,256,128]{2,1,0:T(8,128)(2,1)} %shard_map.86), calls=%async_computation.2 | async-start | bytes 4194304 | tf_op jit(solution)/shard_map/all_to_all | solution.py:348
  71.4 9.6 %shard_map.89 = (bf16[16,128]{1,0:T(8,128)(2,1)}, f32[2,128]{1,0:T(2,128)}, f32[2,128,128]{2,1,0:T(8,128)}) custom-call(bf16[512,128]{1,0:T(8,128)(2,1)S(1)} %bitcast.13, bf16[4096,128]{1,0:T(8,128)(2,1)} %get-tuple-element.67.kv0_ref, bf16[4096,128]{1,0:T(8,128)(2,1)} %get-tuple-element.71.kv1_ref), custom_call_target="tpu_custom_call" | custom-call | flops 8000000000 | bytes 1000000 | tf_op jit(solution)/shard_map/pallas_call | solution.py:336
  84.9 35.5 %all-to-all-done.2.two_ref = bf16[32,256,128]{2,1,0:T(8,128)(2,1)S(1)} async-done(((bf16[32,256,128]{2,1,0:T(8,128)(2,1)}), bf16[32,256,128]{2,1,0:T(8,128)(2,1)S(1)}, u32[]{:S(2)}, u32[]{:S(2)}) %all-to-all-start.2) | async-done | bytes 2097184 | tf_op jit(solution)/shard_map/all_to_all | solution.py:348
  121.8 5.6 %all-to-all-start.3 = ((bf16[32,400,128]{2,1,0:T(8,128)(2,1)}), bf16[32,400,128]{2,1,0:T(8,128)(2,1)S(1)}, u32[]{:S(2)}, u32[]{:S(2)}) async-start(bf16[32,400,128]{2,1,0:T(8,128)(2,1)} %shard_map.90), calls=%async_computation.3 | async-start | bytes 6553600 | tf_op jit(solution)/shard_map/all_to_all | solution.py:348
  127.4 6.2 %shard_map.87 = (bf16[4096,128]{1,0:T(8,128)(2,1)}, bf16[4096,128]{1,0:T(8,128)(2,1)}) custom-call(bf16[4096,128]{1,0:T(8,128)(2,1)} %a_ref.2, bf16[4096,128]{1,0:T(8,128)(2,1)} %b_ref.2), custom_call_target="tpu_custom_call" | custom-call | tf_op jit(solution)/shard_map/pallas_call | solution.py:402
  134.9 41.3 %shard_map.91 = (bf16[32,128,128]{2,1,0:T(8,128)(2,1)}, bf16[32,384,128]{2,1,0:T(8,128)(2,1)}, f32[34,128,128]{2,1,0:T(8,128)}, bf16[2,128,128]{2,1,0:T(8,128)(2,1)}, f32[128,128]{1,0:T(8,128)}) custom-call(s32[64]{0:T(128)S(1)} %multiply_add_fusion.slot_ref, s32[2]{0:T(128)S(1)} %add_convert_fusion.edge_ref, bf16[32,128,128]{2,1,0:T(8,128)(2,1)} %bitcast.23, ...), custom_call_target="tpu_custom_call" | custom-call | flops 38000001024 | bytes 1000000 | tf_op jit(solution)/shard_map/pallas_call | solution.py:336
  176.2 23.4 %all-to-all-done.3.three_ref = bf16[32,400,128]{2,1,0:T(8,128)(2,1)S(1)} async-done(((bf16[32,400,128]{2,1,0:T(8,128)(2,1)}), bf16[32,400,128]{2,1,0:T(8,128)(2,1)S(1)}, u32[]{:S(2)}, u32[]{:S(2)}) %all-to-all-start.3) | async-done | bytes 3276832 | tf_op jit(solution)/shard_map/all_to_all | solution.py:348
  199.6 6.7 %all-to-all-start.4 = ((bf16[32,384,128]{2,1,0:T(8,128)(2,1)}), bf16[32,384,128]{2,1,0:T(8,128)(2,1)}, u32[]{:S(2)}, u32[]{:S(2)}) async-start(bf16[32,384,128]{2,1,0:T(8,128)(2,1)} %get-tuple-element.92), calls=%async_computation.4 | async-start | bytes 6291456 | tf_op jit(solution)/shard_map/all_to_all | solution.py:348
  206.3 10.5 %shard_map.92 = (f32[4096,128]{1,0:T(8,128)}, f32[4096,128]{1,0:T(8,128)}, f32[2,128,128]{2,1,0:T(8,128)}) custom-call(bf16[512,128]{1,0:T(8,128)(2,1)S(1)} %bitcast.15, bf16[4096,128]{1,0:T(8,128)(2,1)} %get-tuple-element.67.kv0_ref, bf16[4096,128]{1,0:T(8,128)(2,1)} %get-tuple-element.71.kv1_ref, bf16[32,16,128]{2,1,0:T(8,128)(2,1)S(1)} %slice.52.all_ref, ...), custom_call_target="tpu_custom_call" | custom-call | flops 8000000000 | bytes 1000000 | tf_op jit(solution)/shard_map/pallas_call | solution.py:336
  216.8 41.3 %shard_map.93 = (bf16[32,128,128]{2,1,0:T(8,128)(2,1)}, bf16[32,272,128]{2,1,0:T(8,128)(2,1)}, bf16[32,144,128]{2,1,0:T(8,128)(2,1)}, f32[34,128,128]{2,1,0:T(8,128)}, bf16[2,128,128]{2,1,0:T(8,128)(2,1)}) custom-call(s32[64]{0:T(128)S(1)} %multiply_add_fusion.slot_ref, s32[2]{0:T(128)S(1)} %add_convert_fusion.edge_ref, bf16[32,128,128]{2,1,0:T(8,128)(2,1)} %bitcast.22, ...), custom_call_target="tpu_custom_call" | custom-call | flops 38000001024 | bytes 1000000 | tf_op jit(solution)/shard_map/pallas_call | solution.py:336
  270.4 5.6 %all-to-all-done.4.three_ref = bf16[32,384,128]{2,1,0:T(8,128)(2,1)} async-done(((bf16[32,384,128]{2,1,0:T(8,128)(2,1)}), bf16[32,384,128]{2,1,0:T(8,128)(2,1)}, u32[]{:S(2)}, u32[]{:S(2)}) %all-to-all-start.4) | async-done | bytes 3145760 | tf_op jit(solution)/shard_map/all_to_all | solution.py:348
  276.0 57.0 %all_to_all.35.two_ref = bf16[32,272,128]{2,1,0:T(8,128)(2,1)S(1)} all-to-all(bf16[32,272,128]{2,1,0:T(8,128)(2,1)} %get-tuple-element.97), channel_id=1, replica_groups=mesh['seq'=32,'head'=8] {'seq'}, dimensions={0} | all-to-all | bytes 4456448 | tf_op jit(solution)/shard_map/all_to_all | solution.py:348
  333.8 5.8 %all-to-all-start.6 = ((bf16[32,144,128]{2,1,0:T(8,128)(2,1)}), bf16[32,144,128]{2,1,0:T(8,128)(2,1)S(1)}, u32[]{:S(2)}, u32[]{:S(2)}) async-start(bf16[32,144,128]{2,1,0:T(8,128)(2,1)} %broadcast_dynamic-update-slice_fusion), calls=%async_computation.6 | async-start | bytes 2359296 | tf_op jit(solution)/shard_map/all_to_all | solution.py:348
  339.6 5.7 %shard_map.96 = (bf16[32,128,128]{2,1,0:T(8,128)(2,1)}, bf16[32,128,128]{2,1,0:T(8,128)(2,1)}) custom-call(bf16[32,128,128]{2,1,0:T(8,128)(2,1)} %get-tuple-element.104.od0_ref, bf16[32,128,128]{2,1,0:T(8,128)(2,1)} %get-tuple-element.105.od1_ref), custom_call_target="tpu_custom_call" | custom-call | flops 4000000000 | bytes 1000000 | tf_op jit(solution)/shard_map/pallas_call | solution.py:336
  345.2 5.3 %shard_map.95 = (bf16[32,128,128]{2,1,0:T(8,128)(2,1)}, f32[128,128]{1,0:T(8,128)}) custom-call(s32[96]{0:T(128)S(1)} %reshape.188.wanted_ref, f32[34,128,128]{2,1,0:T(8,128)} %get-tuple-element.99.acc_ref, f32[4096,128]{1,0:T(8,128)} %get-tuple-element.100.far_ref, bf16[2,128,128]{2,1,0:T(8,128)(2,1)S(1)} %collective-permute-done.2.left_ref, ...), custom_call_target="tpu_custom_call" | custom-call | flops 6000000000 | bytes 1000000 | tf_op jit(solution)/shard_map/pallas_call | solution.py:336
  350.5 4.5 %shard_map.94.part_ref = f32[32,128,128]{2,1,0:T(8,128)} custom-call(s32[96]{0:T(128)S(1)} %reshape.188.wanted_ref, f32[34,128,128]{2,1,0:T(8,128)} %get-tuple-element.89.acc_ref, f32[4096,128]{1,0:T(8,128)} %get-tuple-element.90.far_ref, bf16[2,128,128]{2,1,0:T(8,128)(2,1)S(1)} %collective-permute-done.2.left_ref, ...), custom_call_target="tpu_custom_call" | custom-call | flops 4000000000 | bytes 1000000 | tf_op jit(solution)/shard_map/pallas_call | solution.py:336
  355.0 11.3 %all-to-all-done.6.late_ref = bf16[32,144,128]{2,1,0:T(8,128)(2,1)S(1)} async-done(((bf16[32,144,128]{2,1,0:T(8,128)(2,1)}), bf16[32,144,128]{2,1,0:T(8,128)(2,1)S(1)}, u32[]{:S(2)}, u32[]{:S(2)}) %all-to-all-start.6) | async-done | bytes 1179680 | tf_op jit(solution)/shard_map/all_to_all | solution.py:348
  366.3 6.1 %shard_map.97 = (bf16[32,128,128]{2,1,0:T(8,128)(2,1)}, bf16[32,128,128]{2,1,0:T(8,128)(2,1)}, bf16[4096,128]{1,0:T(8,128)(2,1)}, bf16[4096,128]{1,0:T(8,128)(2,1)}) custom-call(s32[96]{0:T(128)S(1)} %reshape.188.wanted_ref, s32[2]{0:T(128)S(1)} %add_convert_fusion.edge_ref, ...), custom_call_target="tpu_custom_call", output_to_operand_aliasing={{2}: (6, {}), {3}: (7, {})} | custom-call | flops 4000000000 | bytes 1000000 | tf_op jit(solution)/shard_map/pallas_call | solution.py:528
  (47 shorter events, 34.7 us)
Async XLA Ops:
  3.6 22.8 %all-to-all-start = ((bf16[32,32,128]{2,1,0:T(8,128)(2,1)}), bf16[32,32,128]{2,1,0:T(8,128)(2,1)S(1)}, u32[]{:S(2)}, u32[]{:S(2)}) async-start(bf16[32,32,128]{2,1,0:T(8,128)(2,1)} %get-tuple-element.64), calls=%async_computation | async-start | bytes 524288 | tf_op jit(solution)/shard_map/all_to_all | solution.py:348
  29.5 35.6 %all-to-all-start.1 = ((bf16[32,144,128]{2,1,0:T(8,128)(2,1)}), bf16[32,144,128]{2,1,0:T(8,128)(2,1)S(1)}, u32[]{:S(2)}, u32[]{:S(2)}) async-start(bf16[32,144,128]{2,1,0:T(8,128)(2,1)} %shard_map.88), calls=%async_computation.1 | async-start | bytes 2359296 | tf_op jit(solution)/shard_map/all_to_all | solution.py:348
  35.1 2.9 copy-start.7
  35.1 6.2 %copy-start.6 = (bf16[2,128,128]{2,1,0:T(8,128)(2,1)S(1)}, bf16[2,128,128]{2,1,0:T(8,128)(2,1)}, u32[]{:S(2)}) copy-start(bf16[2,128,128]{2,1,0:T(8,128)(2,1)} %get-tuple-element.74) | copy-start | bytes 196612
  38.0 6.2 %collective-permute-start = (bf16[2,128,128]{2,1,0:T(8,128)(2,1)S(1)}, bf16[2,128,128]{2,1,0:T(8,128)(2,1)S(1)}, u32[]{:S(2)}, u32[]{:S(2)}) collective-permute-start(bf16[2,128,128]{2,1,0:T(8,128)(2,1)S(1)} %copy-done.7), channel_id=1, source_target_pairs={{0,8},{8,16},{16,24},{24,32},{32,40},{40,48},{48,56},{56,64},{64,7... | collective-permute-start | bytes 196616 | tf_op jit(solution)/shard_map/ppermute | solution.py:434
  41.3 6.8 %collective-permute-start.1 = (bf16[2,128,128]{2,1,0:T(8,128)(2,1)S(1)}, bf16[2,128,128]{2,1,0:T(8,128)(2,1)S(1)}, u32[]{:S(2)}, u32[]{:S(2)}) collective-permute-start(bf16[2,128,128]{2,1,0:T(8,128)(2,1)S(1)} %copy-done.6), channel_id=1, source_target_pairs={{8,0},{16,8},{24,16},{32,24},{40,32},{48,40},{56,48},{64,56},{72,6... | collective-permute-start | bytes 196616 | tf_op jit(solution)/shard_map/ppermute | solution.py:435
  65.1 6.3 %copy-start.2 = (bf16[32,144,128]{2,1,0:T(8,128)(2,1)}, bf16[32,144,128]{2,1,0:T(8,128)(2,1)S(1)}, u32[]{:S(2)}) copy-start(bf16[32,144,128]{2,1,0:T(8,128)(2,1)S(1)} %all-to-all-done.1.one_ref) | copy-start | bytes 3538948
  65.1 55.3 %all-to-all-start.2 = ((bf16[32,256,128]{2,1,0:T(8,128)(2,1)}), bf16[32,256,128]{2,1,0:T(8,128)(2,1)S(1)}, u32[]{:S(2)}, u32[]{:S(2)}) async-start(bf16[32,256,128]{2,1,0:T(8,128)(2,1)} %shard_map.86), calls=%async_computation.2 | async-start | bytes 4194304 | tf_op jit(solution)/shard_map/all_to_all | solution.py:348
  81.1 0.7 copy-start.4
  120.4 1.3 copy-start
  121.8 77.8 %all-to-all-start.3 = ((bf16[32,400,128]{2,1,0:T(8,128)(2,1)}), bf16[32,400,128]{2,1,0:T(8,128)(2,1)S(1)}, u32[]{:S(2)}, u32[]{:S(2)}) async-start(bf16[32,400,128]{2,1,0:T(8,128)(2,1)} %shard_map.90), calls=%async_computation.3 | async-start | bytes 6553600 | tf_op jit(solution)/shard_map/all_to_all | solution.py:348
  127.4 6.3 %copy-start.1 = (bf16[32,256,128]{2,1,0:T(8,128)(2,1)S(1)}, bf16[32,256,128]{2,1,0:T(8,128)(2,1)}, u32[]{:S(2)}) copy-start(bf16[32,256,128]{2,1,0:T(8,128)(2,1)} %copy-done) | copy-start | bytes 6291460
  133.6 1.3 copy-start.3
  199.6 76.4 %all-to-all-start.4 = ((bf16[32,384,128]{2,1,0:T(8,128)(2,1)}), bf16[32,384,128]{2,1,0:T(8,128)(2,1)}, u32[]{:S(2)}, u32[]{:S(2)}) async-start(bf16[32,384,128]{2,1,0:T(8,128)(2,1)} %get-tuple-element.92), calls=%async_computation.4 | async-start | bytes 6291456 | tf_op jit(solution)/shard_map/all_to_all | solution.py:348
  216.8 41.3 %copy-start.5 = (bf16[2,128,128]{2,1,0:T(8,128)(2,1)S(1)}, bf16[2,128,128]{2,1,0:T(8,128)(2,1)}, u32[]{:S(2)}) copy-start(bf16[2,128,128]{2,1,0:T(8,128)(2,1)} %get-tuple-element.93) | copy-start | bytes 196612
  258.8 8.0 %collective-permute-start.2 = (bf16[2,128,128]{2,1,0:T(8,128)(2,1)S(1)}, bf16[2,128,128]{2,1,0:T(8,128)(2,1)S(1)}, u32[]{:S(2)}, u32[]{:S(2)}) collective-permute-start(bf16[2,128,128]{2,1,0:T(8,128)(2,1)S(1)} %pad_maximum_fusion), channel_id=1, source_target_pairs={{0,8},{8,16},{16,24},{24,32},{32,40},{40,48},{48,56},{56,64},{64,7... | collective-permute-start | bytes 196616 | tf_op jit(solution)/shard_map/ppermute | solution.py:499
  262.2 8.1 %collective-permute-start.3 = (bf16[2,128,128]{2,1,0:T(8,128)(2,1)S(1)}, bf16[2,128,128]{2,1,0:T(8,128)(2,1)S(1)}, u32[]{:S(2)}, u32[]{:S(2)}) collective-permute-start(bf16[2,128,128]{2,1,0:T(8,128)(2,1)S(1)} %pad_maximum_fusion.1), channel_id=1, source_target_pairs={{8,0},{16,8},{24,16},{32,24},{40,32},{48,40},{56,48},{64,56},{72,6... | collective-permute-start | bytes 196616 | tf_op jit(solution)/shard_map/ppermute | solution.py:500
  333.8 32.5 %all-to-all-start.6 = ((bf16[32,144,128]{2,1,0:T(8,128)(2,1)}), bf16[32,144,128]{2,1,0:T(8,128)(2,1)S(1)}, u32[]{:S(2)}, u32[]{:S(2)}) async-start(bf16[32,144,128]{2,1,0:T(8,128)(2,1)} %broadcast_dynamic-update-slice_fusion), calls=%async_computation.6 | async-start | bytes 2359296 | tf_op jit(solution)/shard_map/all_to_all | solution.py:348

commit v4 on v3

--- a/solution.py
+++ b/solution.py
@@ -56,11 +56,12 @@
 
 
 def gather0_kernel(wanted_ref, kv_ref, piece_ref, out_ref):
-    count = out_ref.shape[0]
-    start = pl.program_id(0) * count
-    for d in range(count):
-        out_ref[d, :BLOCK] = kv_ref[wanted_ref[CAP * (start + d)]]
+    def copy(d, _):
+        out_ref[d, :BLOCK] = kv_ref[wanted_ref[CAP * d]]
         out_ref[d, BLOCK:] = piece_ref[...]
+        return 0
+
+    lax.fori_loop(0, out_ref.shape[0], copy, 0, unroll=4)
 
 
 def gather0_rest_kernel(wanted_ref, kv_ref, out_ref):
@@ -292,6 +293,7 @@
     dk_ref, dv_ref, att_out, dq_out, add_ref,
 ):
     step, count = pl.program_id(0), dk_ref.shape[0]
+    keep = edge_ref[0].astype(F32)
 
     @pl.when(step == 0)
     def _():
@@ -302,22 +304,21 @@
             return 0
 
         lax.fori_loop(0, late_ref.shape[0], add, 0)
+        add_ref[0] += late_ref[:, BLOCK:].reshape(4 * BLOCK, BLOCK)[3 * BLOCK :].astype(F32) * keep
+
+    for b in range(count):
+        dk_ref[b], dv_ref[b] = join(head0_ref[b], part_ref[b] + add_ref[step * count + b])
+
+    @pl.when(step == 0)
+    def _():
         is_first = edge_ref[0] == 1
         root = late_ref[:, BLOCK:].reshape(4 * BLOCK, BLOCK).astype(F32)
         root = [root[i * BLOCK : (i + 1) * BLOCK] for i in range(4)]
-        add_ref[0] += root[3] * edge_ref[0].astype(F32)
         dk_ref[0], dv_ref[0] = join(
-            block_ref[...] + root[2] * edge_ref[0].astype(F32), part_ref[0] + add_ref[0]
+            block_ref[...] + root[2] * keep, part_ref[0] + add_ref[0]
         )
         for new, old_ref, out_ref in zip(join(root[0], root[1]), (dq_ref, att_ref), (dq_out, att_out)):
             out_ref[...] = jnp.where(is_first, new.astype(F32), old_ref[...].astype(F32)).astype(BF16)
-
-    for b in range(count):
-        at = step * count + b
-
-        @pl.when(at > 0)
-        def _(b=b, at=at):
-            dk_ref[b], dv_ref[b] = join(head0_ref[b], part_ref[b] + add_ref[at])
 
 
 def unpack_kernel(od0_ref, od1_ref, att_ref, dq_ref):
@@ -371,7 +372,7 @@
     asked = jnp.sum(
         jnp.where(slot_of[None, :] == jnp.arange(slots)[:, None], inner[None, :], 0), axis=1
     ).reshape(shards, 1, CAP)
-    asked = jnp.pad(asked.astype(BF16), ((0, 0), (0, 15), (0, BLOCK - CAP)))
+    asked = jnp.pad(asked.astype(BF16), ((0, 0), (0, 7), (0, BLOCK - CAP)))
     top = pl.BlockSpec(tile, lambda i: (0, 0))
     end = pl.BlockSpec(tile, lambda i: (blocks - 1, 0))
     query, key, value, grad_out = (in_hbm(x) for x in (query, key, value, grad_out))
@@ -379,13 +380,13 @@
         ask_kernel,
         grid=(1,),
         out_shape=[
-            pltpu.HBM((shards, extra + 16, BLOCK), BF16),
+            pltpu.HBM((shards, extra + 8, BLOCK), BF16),
             pltpu.HBM((2, *tile), BF16),
             pltpu.HBM((2, *tile), BF16),
         ],
         in_specs=[pl.BlockSpec(asked.shape, lambda i: (0, 0, 0)), top, top, top, top, end, end],
         out_specs=[
-            pl.BlockSpec((shards, extra + 16, BLOCK), lambda i: (0, 0, 0)),
+            pl.BlockSpec((shards, extra + 8, BLOCK), lambda i: (0, 0, 0)),
             pl.BlockSpec((2, *tile), lambda i: (0, 0, 0)),
             pl.BlockSpec((2, *tile), lambda i: (0, 0, 0)),
         ],
@@ -410,18 +411,13 @@
 
     kv0, kv1 = pack(key, value)
     steps = 4
-    one0 = pl.pallas_call(
+    (one0,) = call(
         gather0_kernel,
-        grid=(steps,),
-        out_shape=pltpu.HBM((shards, BLOCK + extra, BLOCK), BF16),
-        in_specs=[
-            in_smem,
-            pl.BlockSpec(grid, lambda i: (0, 0, 0)),
-            pl.BlockSpec((extra, BLOCK), lambda i: (0, 0)),
-        ],
-        out_specs=pl.BlockSpec((shards // steps, BLOCK + extra, BLOCK), lambda i: (i, 0, 0)),
-        compiler_params=params(),
-    )(wanted, in_hbm(kv0.reshape(grid)), got[0, :extra])
+        [((shards, BLOCK + extra, BLOCK), BF16)],
+        (wanted, kv0.reshape(grid), got[0, :extra]),
+        smem=1,
+        loose=(2,),
+    )
     (two0,) = call(
         gather0_rest_kernel,
         [((shards, 2 * BLOCK, BLOCK), BF16)],

time: 374 us -> 374 us (level)
    pallas_call x9 -> x10, Pallas kernels: 124 us -> 127 us  [call(): pl.pallas_call(kernel, out_shape=[pltpu.HBM(s, d) for s, d in outs], in_s...]
where the time goes in v4:
time: 374 us; the launch traced here: 372 us
  Pallas kernels  145 us (39%)
  waiting for transfers between devices  109 us (29%)
  blocking collectives  56.6 us (15%)
  starting transfers between devices  53.8 us (14%)
  local copies, waits for them, and re-layouts  5.93 us (2%)
    pallas_call x10, Pallas kernels, call(): pl.pallas_call(kernel, out_shape=[pltpu.HBM(s, d) for s, d in outs], in_s...  127 us
    all_to_all x6, waiting for transfers between devices, exchange(): lax.all_to_all(blocks, 'seq', split_axis=0, concat_axis=0, tiled=True)  99.9 us
    all_to_all x1, blocking collectives, exchange(): lax.all_to_all(blocks, 'seq', split_axis=0, concat_axis=0, tiled=True)  56.6 us
    all_to_all x6, starting transfers between devices, exchange(): lax.all_to_all(blocks, 'seq', split_axis=0, concat_axis=0, tiled=True)  42.1 us
    pallas_call x2, Pallas kernels, pack(): pl.pallas_call(pack_kernel, grid=(rows // chunk,), out_shape=[pltpu.HBM((...  12.3 us
  transfers between devices with their start and end apart: 10, of which 10 were waited for; matrix products, arithmetic and copies ran while one was open for 0% of the time, Pallas kernels for 37%

profile of v4, /device:TPU:2, one launch (start us, length us, event | category | flops | bytes accessed | tf_op | source)
XLA Modules:
  0.0 372.0 jit_solution(525533151493257743)
XLA Ops:
  3.6 11.6 %all-to-all-start = ((bf16[32,24,128]{2,1,0:T(8,128)(2,1)}), bf16[32,24,128]{2,1,0:T(8,128)(2,1)S(1)}, u32[]{:S(2)}, u32[]{:S(2)}) async-start(bf16[32,24,128]{2,1,0:T(8,128)(2,1)} %get-tuple-element.64), calls=%async_computation | async-start | bytes 393216 | tf_op jit(solution)/shard_map/all_to_all | solution.py:349
  15.2 6.1 %shard_map.85 = (bf16[4096,128]{1,0:T(8,128)(2,1)}, bf16[4096,128]{1,0:T(8,128)(2,1)}) custom-call(bf16[4096,128]{1,0:T(8,128)(2,1)} %a_ref.1, bf16[4096,128]{1,0:T(8,128)(2,1)} %b_ref.1), custom_call_target="tpu_custom_call" | custom-call | tf_op jit(solution)/shard_map/pallas_call | solution.py:403
  21.3 3.7 %all-to-all-done = bf16[32,24,128]{2,1,0:T(8,128)(2,1)S(1)} async-done(((bf16[32,24,128]{2,1,0:T(8,128)(2,1)}), bf16[32,24,128]{2,1,0:T(8,128)(2,1)S(1)}, u32[]{:S(2)}, u32[]{:S(2)}) %all-to-all-start) | async-done | bytes 196640 | tf_op jit(solution)/shard_map/all_to_all | solution.py:349
  27.6 6.0 %all-to-all-start.1 = ((bf16[32,144,128]{2,1,0:T(8,128)(2,1)}), bf16[32,144,128]{2,1,0:T(8,128)(2,1)S(1)}, u32[]{:S(2)}, u32[]{:S(2)}) async-start(bf16[32,144,128]{2,1,0:T(8,128)(2,1)} %shard_map.88), calls=%async_computation.1 | async-start | bytes 2359296 | tf_op jit(solution)/shard_map/all_to_all | solution.py:349
  42.8 4.0 %collective-permute-done.1.high_ref = bf16[2,128,128]{2,1,0:T(8,128)(2,1)S(1)} collective-permute-done((bf16[2,128,128]{2,1,0:T(8,128)(2,1)S(1)}, bf16[2,128,128]{2,1,0:T(8,128)(2,1)S(1)}, u32[]{:S(2)}, u32[]{:S(2)}) %collective-permute-start.1) | collective-permute-done | bytes 65568 | tf_op jit(solution)/shard_map/ppermute | solution.py:431
  46.8 17.2 %all-to-all-done.1.one_ref = bf16[32,144,128]{2,1,0:T(8,128)(2,1)S(1)} async-done(((bf16[32,144,128]{2,1,0:T(8,128)(2,1)}), bf16[32,144,128]{2,1,0:T(8,128)(2,1)S(1)}, u32[]{:S(2)}, u32[]{:S(2)}) %all-to-all-start.1) | async-done | bytes 1179680 | tf_op jit(solution)/shard_map/all_to_all | solution.py:349
  63.9 6.3 %all-to-all-start.2 = ((bf16[32,256,128]{2,1,0:T(8,128)(2,1)}), bf16[32,256,128]{2,1,0:T(8,128)(2,1)S(1)}, u32[]{:S(2)}, u32[]{:S(2)}) async-start(bf16[32,256,128]{2,1,0:T(8,128)(2,1)} %shard_map.86), calls=%async_computation.2 | async-start | bytes 4194304 | tf_op jit(solution)/shard_map/all_to_all | solution.py:349
  70.2 9.6 %shard_map.89 = (bf16[16,128]{1,0:T(8,128)(2,1)}, f32[2,128]{1,0:T(2,128)}, f32[2,128,128]{2,1,0:T(8,128)}) custom-call(bf16[512,128]{1,0:T(8,128)(2,1)S(1)} %bitcast.13, bf16[4096,128]{1,0:T(8,128)(2,1)} %get-tuple-element.67.kv0_ref, bf16[4096,128]{1,0:T(8,128)(2,1)} %get-tuple-element.71.kv1_ref), custom_call_target="tpu_custom_call" | custom-call | flops 8000000000 | bytes 1000000 | tf_op jit(solution)/shard_map/pallas_call | solution.py:337
  83.8 35.0 %all-to-all-done.2.two_ref = bf16[32,256,128]{2,1,0:T(8,128)(2,1)S(1)} async-done(((bf16[32,256,128]{2,1,0:T(8,128)(2,1)}), bf16[32,256,128]{2,1,0:T(8,128)(2,1)S(1)}, u32[]{:S(2)}, u32[]{:S(2)}) %all-to-all-start.2) | async-done | bytes 2097184 | tf_op jit(solution)/shard_map/all_to_all | solution.py:349
  120.1 6.5 %all-to-all-start.3 = ((bf16[32,400,128]{2,1,0:T(8,128)(2,1)}), bf16[32,400,128]{2,1,0:T(8,128)(2,1)S(1)}, u32[]{:S(2)}, u32[]{:S(2)}) async-start(bf16[32,400,128]{2,1,0:T(8,128)(2,1)} %shard_map.90), calls=%async_computation.3 | async-start | bytes 6553600 | tf_op jit(solution)/shard_map/all_to_all | solution.py:349
  126.7 6.2 %shard_map.87 = (bf16[4096,128]{1,0:T(8,128)(2,1)}, bf16[4096,128]{1,0:T(8,128)(2,1)}) custom-call(bf16[4096,128]{1,0:T(8,128)(2,1)} %a_ref.2, bf16[4096,128]{1,0:T(8,128)(2,1)} %b_ref.2), custom_call_target="tpu_custom_call" | custom-call | tf_op jit(solution)/shard_map/pallas_call | solution.py:403
  134.2 41.3 %shard_map.91 = (bf16[32,128,128]{2,1,0:T(8,128)(2,1)}, bf16[32,384,128]{2,1,0:T(8,128)(2,1)}, f32[34,128,128]{2,1,0:T(8,128)}, bf16[2,128,128]{2,1,0:T(8,128)(2,1)}, f32[128,128]{1,0:T(8,128)}) custom-call(s32[64]{0:T(128)S(1)} %multiply_add_fusion.slot_ref, s32[2]{0:T(128)S(1)} %add_convert_fusion.edge_ref, bf16[32,128,128]{2,1,0:T(8,128)(2,1)} %bitcast.23, ...), custom_call_target="tpu_custom_call" | custom-call | flops 38000001024 | bytes 1000000 | tf_op jit(solution)/shard_map/pallas_call | solution.py:337
  175.5 25.2 %all-to-all-done.3.three_ref = bf16[32,400,128]{2,1,0:T(8,128)(2,1)S(1)} async-done(((bf16[32,400,128]{2,1,0:T(8,128)(2,1)}), bf16[32,400,128]{2,1,0:T(8,128)(2,1)S(1)}, u32[]{:S(2)}, u32[]{:S(2)}) %all-to-all-start.3) | async-done | bytes 3276832 | tf_op jit(solution)/shard_map/all_to_all | solution.py:349
  200.7 5.9 %all-to-all-start.4 = ((bf16[32,384,128]{2,1,0:T(8,128)(2,1)}), bf16[32,384,128]{2,1,0:T(8,128)(2,1)}, u32[]{:S(2)}, u32[]{:S(2)}) async-start(bf16[32,384,128]{2,1,0:T(8,128)(2,1)} %get-tuple-element.92), calls=%async_computation.4 | async-start | bytes 6291456 | tf_op jit(solution)/shard_map/all_to_all | solution.py:349
  206.5 10.5 %shard_map.92 = (f32[4096,128]{1,0:T(8,128)}, f32[4096,128]{1,0:T(8,128)}, f32[2,128,128]{2,1,0:T(8,128)}) custom-call(bf16[512,128]{1,0:T(8,128)(2,1)S(1)} %bitcast.15, bf16[4096,128]{1,0:T(8,128)(2,1)} %get-tuple-element.67.kv0_ref, bf16[4096,128]{1,0:T(8,128)(2,1)} %get-tuple-element.71.kv1_ref, bf16[32,16,128]{2,1,0:T(8,128)(2,1)S(1)} %slice.52.all_ref, ...), custom_call_target="tpu_custom_call" | custom-call | flops 8000000000 | bytes 1000000 | tf_op jit(solution)/shard_map/pallas_call | solution.py:337
  217.0 41.3 %shard_map.93 = (bf16[32,128,128]{2,1,0:T(8,128)(2,1)}, bf16[32,272,128]{2,1,0:T(8,128)(2,1)}, bf16[32,144,128]{2,1,0:T(8,128)(2,1)}, f32[34,128,128]{2,1,0:T(8,128)}, bf16[2,128,128]{2,1,0:T(8,128)(2,1)}) custom-call(s32[64]{0:T(128)S(1)} %multiply_add_fusion.slot_ref, s32[2]{0:T(128)S(1)} %add_convert_fusion.edge_ref, bf16[32,128,128]{2,1,0:T(8,128)(2,1)} %bitcast.22, ...), custom_call_target="tpu_custom_call" | custom-call | flops 38000001024 | bytes 1000000 | tf_op jit(solution)/shard_map/pallas_call | solution.py:337
  269.5 7.4 %all-to-all-done.4.three_ref = bf16[32,384,128]{2,1,0:T(8,128)(2,1)} async-done(((bf16[32,384,128]{2,1,0:T(8,128)(2,1)}), bf16[32,384,128]{2,1,0:T(8,128)(2,1)}, u32[]{:S(2)}, u32[]{:S(2)}) %all-to-all-start.4) | async-done | bytes 3145760 | tf_op jit(solution)/shard_map/all_to_all | solution.py:349
  276.8 56.6 %all_to_all.35.two_ref = bf16[32,272,128]{2,1,0:T(8,128)(2,1)S(1)} all-to-all(bf16[32,272,128]{2,1,0:T(8,128)(2,1)} %get-tuple-element.97), channel_id=1, replica_groups=mesh['seq'=32,'head'=8] {'seq'}, dimensions={0} | all-to-all | bytes 4456448 | tf_op jit(solution)/shard_map/all_to_all | solution.py:349
  334.2 5.8 %all-to-all-start.6 = ((bf16[32,144,128]{2,1,0:T(8,128)(2,1)}), bf16[32,144,128]{2,1,0:T(8,128)(2,1)S(1)}, u32[]{:S(2)}, u32[]{:S(2)}) async-start(bf16[32,144,128]{2,1,0:T(8,128)(2,1)} %broadcast_dynamic-update-slice_fusion), calls=%async_computation.6 | async-start | bytes 2359296 | tf_op jit(solution)/shard_map/all_to_all | solution.py:349
  340.0 5.7 %shard_map.96 = (bf16[32,128,128]{2,1,0:T(8,128)(2,1)}, bf16[32,128,128]{2,1,0:T(8,128)(2,1)}) custom-call(bf16[32,128,128]{2,1,0:T(8,128)(2,1)} %get-tuple-element.104.od0_ref, bf16[32,128,128]{2,1,0:T(8,128)(2,1)} %get-tuple-element.105.od1_ref), custom_call_target="tpu_custom_call" | custom-call | flops 4000000000 | bytes 1000000 | tf_op jit(solution)/shard_map/pallas_call | solution.py:337
  345.7 5.3 %shard_map.95 = (bf16[32,128,128]{2,1,0:T(8,128)(2,1)}, f32[128,128]{1,0:T(8,128)}) custom-call(s32[96]{0:T(128)S(1)} %reshape.188.wanted_ref, f32[34,128,128]{2,1,0:T(8,128)} %get-tuple-element.99.acc_ref, f32[4096,128]{1,0:T(8,128)} %get-tuple-element.100.far_ref, bf16[2,128,128]{2,1,0:T(8,128)(2,1)S(1)} %collective-permute-done.2.left_ref, ...), custom_call_target="tpu_custom_call" | custom-call | flops 6000000000 | bytes 1000000 | tf_op jit(solution)/shard_map/pallas_call | solution.py:337
  351.0 4.5 %shard_map.94.part_ref = f32[32,128,128]{2,1,0:T(8,128)} custom-call(s32[96]{0:T(128)S(1)} %reshape.188.wanted_ref, f32[34,128,128]{2,1,0:T(8,128)} %get-tuple-element.89.acc_ref, f32[4096,128]{1,0:T(8,128)} %get-tuple-element.90.far_ref, bf16[2,128,128]{2,1,0:T(8,128)(2,1)S(1)} %collective-permute-done.2.left_ref, ...), custom_call_target="tpu_custom_call" | custom-call | flops 4000000000 | bytes 1000000 | tf_op jit(solution)/shard_map/pallas_call | solution.py:337
  355.5 11.5 %all-to-all-done.6.late_ref = bf16[32,144,128]{2,1,0:T(8,128)(2,1)S(1)} async-done(((bf16[32,144,128]{2,1,0:T(8,128)(2,1)}), bf16[32,144,128]{2,1,0:T(8,128)(2,1)S(1)}, u32[]{:S(2)}, u32[]{:S(2)}) %all-to-all-start.6) | async-done | bytes 1179680 | tf_op jit(solution)/shard_map/all_to_all | solution.py:349
  366.9 5.0 %shard_map.97 = (bf16[32,128,128]{2,1,0:T(8,128)(2,1)}, bf16[32,128,128]{2,1,0:T(8,128)(2,1)}, bf16[4096,128]{1,0:T(8,128)(2,1)}, bf16[4096,128]{1,0:T(8,128)(2,1)}) custom-call(s32[96]{0:T(128)S(1)} %reshape.188.wanted_ref, s32[2]{0:T(128)S(1)} %add_convert_fusion.edge_ref, ...), custom_call_target="tpu_custom_call", output_to_operand_aliasing={{2}: (6, {}), {3}: (7, {})} | custom-call | flops 4000000000 | bytes 1000000 | tf_op jit(solution)/shard_map/pallas_call | solution.py:524
  (47 shorter events, 33.1 us)
Async XLA Ops:
  3.6 21.4 %all-to-all-start = ((bf16[32,24,128]{2,1,0:T(8,128)(2,1)}), bf16[32,24,128]{2,1,0:T(8,128)(2,1)S(1)}, u32[]{:S(2)}, u32[]{:S(2)}) async-start(bf16[32,24,128]{2,1,0:T(8,128)(2,1)} %get-tuple-element.64), calls=%async_computation | async-start | bytes 393216 | tf_op jit(solution)/shard_map/all_to_all | solution.py:349
  27.6 36.4 %all-to-all-start.1 = ((bf16[32,144,128]{2,1,0:T(8,128)(2,1)}), bf16[32,144,128]{2,1,0:T(8,128)(2,1)S(1)}, u32[]{:S(2)}, u32[]{:S(2)}) async-start(bf16[32,144,128]{2,1,0:T(8,128)(2,1)} %shard_map.88), calls=%async_computation.1 | async-start | bytes 2359296 | tf_op jit(solution)/shard_map/all_to_all | solution.py:349
  33.6 2.9 copy-start.7
  33.6 6.2 %copy-start.6 = (bf16[2,128,128]{2,1,0:T(8,128)(2,1)S(1)}, bf16[2,128,128]{2,1,0:T(8,128)(2,1)}, u32[]{:S(2)}) copy-start(bf16[2,128,128]{2,1,0:T(8,128)(2,1)} %get-tuple-element.74) | copy-start | bytes 196612
  36.5 6.3 %collective-permute-start = (bf16[2,128,128]{2,1,0:T(8,128)(2,1)S(1)}, bf16[2,128,128]{2,1,0:T(8,128)(2,1)S(1)}, u32[]{:S(2)}, u32[]{:S(2)}) collective-permute-start(bf16[2,128,128]{2,1,0:T(8,128)(2,1)S(1)} %copy-done.7), channel_id=1, source_target_pairs={{0,8},{8,16},{16,24},{24,32},{32,40},{40,48},{48,56},{56,64},{64,7... | collective-permute-start | bytes 196616 | tf_op jit(solution)/shard_map/ppermute | solution.py:430
  39.9 6.9 %collective-permute-start.1 = (bf16[2,128,128]{2,1,0:T(8,128)(2,1)S(1)}, bf16[2,128,128]{2,1,0:T(8,128)(2,1)S(1)}, u32[]{:S(2)}, u32[]{:S(2)}) collective-permute-start(bf16[2,128,128]{2,1,0:T(8,128)(2,1)S(1)} %copy-done.6), channel_id=1, source_target_pairs={{8,0},{16,8},{24,16},{32,24},{40,32},{48,40},{56,48},{64,56},{72,6... | collective-permute-start | bytes 196616 | tf_op jit(solution)/shard_map/ppermute | solution.py:431
  63.9 6.3 %copy-start.2 = (bf16[32,144,128]{2,1,0:T(8,128)(2,1)}, bf16[32,144,128]{2,1,0:T(8,128)(2,1)S(1)}, u32[]{:S(2)}) copy-start(bf16[32,144,128]{2,1,0:T(8,128)(2,1)S(1)} %all-to-all-done.1.one_ref) | copy-start | bytes 3538948
  63.9 54.8 %all-to-all-start.2 = ((bf16[32,256,128]{2,1,0:T(8,128)(2,1)}), bf16[32,256,128]{2,1,0:T(8,128)(2,1)S(1)}, u32[]{:S(2)}, u32[]{:S(2)}) async-start(bf16[32,256,128]{2,1,0:T(8,128)(2,1)} %shard_map.86), calls=%async_computation.2 | async-start | bytes 4194304 | tf_op jit(solution)/shard_map/all_to_all | solution.py:349
  79.9 0.7 copy-start.4
  118.7 1.3 copy-start
  120.1 80.6 %all-to-all-start.3 = ((bf16[32,400,128]{2,1,0:T(8,128)(2,1)}), bf16[32,400,128]{2,1,0:T(8,128)(2,1)S(1)}, u32[]{:S(2)}, u32[]{:S(2)}) async-start(bf16[32,400,128]{2,1,0:T(8,128)(2,1)} %shard_map.90), calls=%async_computation.3 | async-start | bytes 6553600 | tf_op jit(solution)/shard_map/all_to_all | solution.py:349
  126.6 6.3 %copy-start.1 = (bf16[32,256,128]{2,1,0:T(8,128)(2,1)S(1)}, bf16[32,256,128]{2,1,0:T(8,128)(2,1)}, u32[]{:S(2)}) copy-start(bf16[32,256,128]{2,1,0:T(8,128)(2,1)} %copy-done) | copy-start | bytes 6291460
  132.9 1.3 copy-start.3
  200.7 76.2 %all-to-all-start.4 = ((bf16[32,384,128]{2,1,0:T(8,128)(2,1)}), bf16[32,384,128]{2,1,0:T(8,128)(2,1)}, u32[]{:S(2)}, u32[]{:S(2)}) async-start(bf16[32,384,128]{2,1,0:T(8,128)(2,1)} %get-tuple-element.92), calls=%async_computation.4 | async-start | bytes 6291456 | tf_op jit(solution)/shard_map/all_to_all | solution.py:349
  217.0 41.3 %copy-start.5 = (bf16[2,128,128]{2,1,0:T(8,128)(2,1)S(1)}, bf16[2,128,128]{2,1,0:T(8,128)(2,1)}, u32[]{:S(2)}) copy-start(bf16[2,128,128]{2,1,0:T(8,128)(2,1)} %get-tuple-element.93) | copy-start | bytes 196612
  259.1 8.0 %collective-permute-start.2 = (bf16[2,128,128]{2,1,0:T(8,128)(2,1)S(1)}, bf16[2,128,128]{2,1,0:T(8,128)(2,1)S(1)}, u32[]{:S(2)}, u32[]{:S(2)}) collective-permute-start(bf16[2,128,128]{2,1,0:T(8,128)(2,1)S(1)} %pad_maximum_fusion), channel_id=1, source_target_pairs={{0,8},{8,16},{16,24},{24,32},{32,40},{40,48},{48,56},{56,64},{64,7... | collective-permute-start | bytes 196616 | tf_op jit(solution)/shard_map/ppermute | solution.py:495
  262.5 7.0 %collective-permute-start.3 = (bf16[2,128,128]{2,1,0:T(8,128)(2,1)S(1)}, bf16[2,128,128]{2,1,0:T(8,128)(2,1)S(1)}, u32[]{:S(2)}, u32[]{:S(2)}) collective-permute-start(bf16[2,128,128]{2,1,0:T(8,128)(2,1)S(1)} %pad_maximum_fusion.1), channel_id=1, source_target_pairs={{8,0},{16,8},{24,16},{32,24},{40,32},{48,40},{56,48},{64,56},{72,6... | collective-permute-start | bytes 196616 | tf_op jit(solution)/shard_map/ppermute | solution.py:496
  334.2 32.7 %all-to-all-start.6 = ((bf16[32,144,128]{2,1,0:T(8,128)(2,1)}), bf16[32,144,128]{2,1,0:T(8,128)(2,1)S(1)}, u32[]{:S(2)}, u32[]{:S(2)}) async-start(bf16[32,144,128]{2,1,0:T(8,128)(2,1)} %broadcast_dynamic-update-slice_fusion), calls=%async_computation.6 | async-start | bytes 2359296 | tf_op jit(solution)/shard_map/all_to_all | solution.py:349
